TPU v7x, 32 devices: a whole 2x2x4 slice. The times are simulated.
32 devices in a mesh: groups: 2 (over y), dp: 4 (over z), layer: 2 (over x), tensor: 2 (over core).
Axes of the slice: x: 2, y: 2, z: 4, core: 2. Of those that a mesh axis runs over, the one named last changes fastest.
Arguments:
- activations: bfloat16 [2, 1536, 14336], P('layer', ('groups', 'dp'), 'tensor'), parts along dimension 1, may hold values from -6 to 6
- out_grads: bfloat16 [2, 1536, 4096], P('layer', ('groups', 'dp'), 'tensor'), parts along dimension 1, may hold values from -6 to 6
- proj_in: bfloat16 [2, 64, 14336], P('layer', None, 'tensor'), may hold values from -0.046875 to 0.046875
- proj_out: bfloat16 [2, 64, 4096], P('layer', None, 'tensor'), may hold values from -0.09375 to 0.09375
- queries: bfloat16 [2, 256, 4096], P('layer', 'dp'), may hold values from -0.0068359375 to 0.0068359375
- lengths: int32 [16], P('groups'), parts along dimension 0, may hold values from 1 to 192, 768 in all
- owner_slot: int32 [16], P('groups'), parts along dimension 0, may hold values from 0 to 7, each once
- pad_mask: int32 [1536], P(('groups', 'dp')), parts along dimension 0, may hold values 0 or 1
Outputs:
- scores: float32 [16, 256], P(('groups', 'dp'), 'layer'), parts along dimension 0
There are 2 independent parts, one for each index of `groups`. A program takes and returns all parts, laid end to end along the dimension named above; an argument that names none is the same for every part. Nothing has to cross between parts.
Inputs may be any that keep to these rules, and one draw needn't show every extreme that they name: `owner_slot`: every output row is the row of exactly one example. The lengths sum to 768; the longest example has exactly 192 tokens.
All inputs are finite; a program needn't handle non-finite values. No bound on the sum of `pad_mask` on one device may be relied on, other than what follows from the above.
Results may differ from a plain program's by a relative error of at most 0.0051.
Values may be sent and summed in bfloat16 or wider, within the bound.
No kernel may reach another device: no remote copies, remote signals or barrier semaphores. Data moves between devices by JAX's collectives and lax.ppermute only.
A program may use at most 64 MiB of HBM per device.

v0:
```python
import jax
import jax.numpy as jnp
from jax import lax
from jax.sharding import PartitionSpec as P


def contract_last(left, right):
    return lax.dot_general(
        left, right, (((1,), (1,)), ((), ())), preferred_element_type=jnp.float32
    )


def spread_scores(local_scores):
    return lax.all_to_all(local_scores, "dp", split_axis=0, concat_axis=1, tiled=True)


def local(activations, out_grads, proj_in, proj_out, queries, lengths, owner_slot, pad_mask):
    tok_rows = activations.shape[1]
    rank_out = proj_out.shape[1]
    example_count = lengths.shape[0]
    inner_side = contract_last(activations[0], proj_in[0])
    outer_side = contract_last(out_grads[0], proj_out[0])
    joined = lax.psum(jnp.concatenate([outer_side, inner_side], axis=1), "tensor")
    grad_side = joined[:, :rank_out].astype(jnp.bfloat16)
    act_side = joined[:, rank_out:].astype(jnp.bfloat16)
    row_start = lax.axis_index("dp") * tok_rows
    positions = row_start + jnp.arange(tok_rows, dtype=jnp.int32)
    example_ends = jnp.cumsum(lengths)
    example_of = jnp.sum((positions[:, None] >= example_ends[None, :]).astype(jnp.int32), axis=1)
    labels = jnp.arange(example_count, dtype=jnp.int32)
    slot_of = jnp.sum(
        jnp.where(example_of[:, None] == labels[None, :], owner_slot[None, :], 0), axis=1
    )
    member = jnp.where(slot_of[:, None] == labels[None, :], pad_mask[:, None], 0).astype(
        jnp.bfloat16
    )
    weighted = (member[:, :, None] * grad_side[:, None, :]).reshape(
        tok_rows, example_count * rank_out
    )
    partial_value = lax.dot_general(
        weighted, act_side, (((0,), (0,)), ((), ())), preferred_element_type=jnp.float32
    )
    partial_value = partial_value.reshape(example_count, -1)
    everyone = lax.psum(partial_value, "dp").astype(jnp.bfloat16)
    scores = spread_scores(contract_last(everyone, queries[0]))
    return lax.psum_scatter(scores, "layer", scatter_dimension=1, tiled=True)


def solution(mesh):
    placed = (
        P("layer", ("groups", "dp"), "tensor"),
        P("layer", ("groups", "dp"), "tensor"),
        P("layer", None, "tensor"),
        P("layer", None, "tensor"),
        P("layer", "dp", None),
        P("groups"),
        P("groups"),
        P(("groups", "dp")),
    )
    return jax.shard_map(
        local, mesh=mesh, in_specs=placed, out_specs=P(("groups", "dp"), "layer"), check_vma=False
    )
```

profile of v0, /device:TPU:0, one launch (start us, length us, event | category | flops | bytes accessed | tf_op | source)
XLA Modules:
  0.0 67.1 jit_solution(10035500347536547203)
XLA Ops:
  6.5 0.0 copy-start
  6.5 0.0 copy-start.1
  6.5 0.0 copy-start.5
  6.5 0.0 copy-start.4
  6.5 0.0 copy-start.3
  6.5 0.0 reduce-scatter.4.cloned.1.call-start
  6.6 0.0 copy-start.2
  6.6 1.8 %copy-done = bf16[1,192,7168]{2,1,0:T(8,128)(2,1)S(1)} copy-done((bf16[1,192,7168]{2,1,0:T(8,128)(2,1)S(1)}, bf16[1,192,7168]{2,1,0:T(8,128)(2,1)}, u32[]{:S(2)}) %copy-start) | copy-done | bytes 2752536
  8.4 2.2 %fusion = f32[192,64]{0,1:T(8,128)S(1)} fusion(bf16[1,192,7168]{2,1,0:T(8,128)(2,1)S(1)} %copy-done, bf16[1,64,7168]{2,1,0:T(8,128)(2,1)} %param.10), kind=kOutput, calls=%fused_computation | convolution fusion | flops 176160768 | bytes 3719168 | tf_op jit(solution)/shard_map/dot_general | solution.py:8
  10.6 0.0 copy-done.1
  10.6 0.0 copy-done.2
  10.6 0.4 fusion.3
  11.0 4.2 %psum.14 = bf16[192,128]{0,1:T(8,128)(2,1)S(1)} all-reduce(f32[192,128]{0,1:T(8,128)S(1)} %pad_maximum_fusion), channel_id=1, replica_groups=mesh['groups'=2,'dp'=4,'layer'=2,'tensor'=2] {'tensor'}, use_global_device_ids=true, to_apply=%region_3.4 | all-reduce | flops 24576 | bytes 147456 | tf_op jit(solution)/shard_map/psum | solution.py:23
  15.2 0.0 copy-done.5
  15.2 0.2 reduce-window.8
  15.4 0.1 convert_reduce_fusion
  15.5 0.0 copy-done.4
  15.5 0.1 select_reduce_fusion
  15.6 0.0 copy-done.3
  15.6 0.2 fusion.8
  15.8 0.1 reshape.82
  16.0 22.7 %all-reduce.1 = bf16[8,4096]{1,0:T(8,128)(2,1)S(1)} all-reduce(f32[8,4096]{1,0:T(8,128)S(1)} %reshape.82), channel_id=1, replica_groups=mesh['groups'=2,'dp'=4,'layer'=2,'tensor'=2] {'dp'}, use_global_device_ids=true, to_apply=%region_4.5 | all-reduce | flops 32768 | bytes 196608 | tf_op jit(solution)/shard_map/psum | solution.py:44
  38.6 0.1 dot_general.17
  38.7 1.3 %fusion.5 = f32[4,2,64]{2,1,0:T(2,128)S(1)} fusion(bf16[4,2,4096]{2,1,0:T(2,128)(2,1)S(1)} %dot_general.17, bf16[1,64,4096]{2,1,0:T(8,128)(2,1)} %param.12), kind=kOutput, calls=%fused_computation.5 | convolution fusion | flops 4194304 | bytes 591872 | tf_op jit(solution)/shard_map/dot_general | solution.py:8
  40.0 0.1 reshape.86
  40.1 7.9 %all_to_all.16 = f32[4,1,128]{2,1,0:T(1,128)S(1)} all-to-all(f32[4,1,128]{2,1,0:T(1,128)S(1)} %reshape.86), channel_id=1, replica_groups=mesh['groups'=2,'dp'=4,'layer'=2,'tensor'=2] {'dp'}, dimensions={0} | all-to-all | bytes 4096 | tf_op jit(solution)/shard_map/all_to_all | solution.py:14
  48.0 0.5 broadcast.39
  48.5 0.7 reduce
  49.2 0.1 reshape.87
  49.3 0.8 %copy.20 = f32[2,4,64]{0,2,1:T(8,128)} copy(f32[2,4,64]{2,0,1:T(2,128)S(1)} %bitcast.29) | data formatting | bytes 4096
  50.0 0.0 reduce-scatter.4.cloned.1.call-update
  50.0 8.7 %reduce-scatter.4.cloned.1.call-done = f32[128,2]{1,0:T(8,128)} async-done(((f32[256,2]{1,0:T(8,128)}), f32[128,2]{1,0:T(8,128)}) %reduce-scatter.4.cloned.1.call-update) | async-done | bytes 1040
  58.8 1.5 %copy.19 = f32[2,128]{1,0:T(2,128)} copy(f32[2,128]{0,1:T(8,128)} %bitcast.28) | data formatting | bytes 2048
  (5 shorter events, 0.1 us)
Async XLA Ops:
  6.5 1.9 %copy-start = (bf16[1,192,7168]{2,1,0:T(8,128)(2,1)S(1)}, bf16[1,192,7168]{2,1,0:T(8,128)(2,1)}, u32[]{:S(2)}) copy-start(bf16[1,192,7168]{2,1,0:T(8,128)(2,1)} %param.8) | copy-start | bytes 8257540
  6.5 4.0 %copy-start.1 = (bf16[1,192,2048]{2,1,0:T(8,128)(2,1)S(1)}, bf16[1,192,2048]{2,1,0:T(8,128)(2,1)}, u32[]{:S(2)}) copy-start(bf16[1,192,2048]{2,1,0:T(8,128)(2,1)} %param.9) | copy-start | bytes 2359300
  6.5 8.7 %copy-start.5 = (s32[8]{0:T(128)S(1)}, s32[8]{0:T(128)}, u32[]{:S(2)}) copy-start(s32[8]{0:T(128)} %param.13) | copy-start | bytes 100
  6.5 8.9 %copy-start.4 = (s32[8]{0:T(128)S(1)}, s32[8]{0:T(128)}, u32[]{:S(2)}) copy-start(s32[8]{0:T(128)} %param.14) | copy-start | bytes 100
  6.5 9.0 %copy-start.3 = (s32[192]{0:T(256)S(1)}, s32[192]{0:T(256)}, u32[]{:S(2)}) copy-start(s32[192]{0:T(256)} %param.15) | copy-start | bytes 2308
  6.5 52.2 %reduce-scatter.4.cloned.1.call-start = ((), (), s32[]{:S(2)}) async-start(), calls=%async_computation.2 | async-start | bytes 196608
  6.6 4.0 %copy-start.2 = (bf16[1,64,2048]{2,1,0:T(8,128)(2,1)S(1)}, bf16[1,64,2048]{2,1,0:T(8,128)(2,1)}, u32[]{:S(2)}) copy-start(bf16[1,64,2048]{2,1,0:T(8,128)(2,1)} %param.11) | copy-start | bytes 786436
Sparse Core Ops, SparseCore 0:
  50.2 8.5 reduce-scatter.3
where the time goes:
time: 67.4 us; the launch traced here: 67.1 us
  blocking collectives  34.7 us (51%)
  between operations  13.5 us (20%)
  waiting for transfers between devices  8.74 us (13%)
  local copies, waits for them, and re-layouts  4.9 us (7%)
  matrix products  4.06 us (6%)
  other arithmetic  1.07 us (2%)
    psum x1, blocking collectives, local(): everyone = lax.psum(partial_value, 'dp').astype(jnp.bfloat16)  22.7 us
    unnamed x2, waiting for transfers between devices  8.74 us
    all_to_all x1, blocking collectives, spread_scores(): lax.all_to_all(local_scores, 'dp', split_axis=0, concat_axis=1, tiled=True)  7.91 us
    unnamed x16, local copies, waits for them, and re-layouts  4.21 us
    psum x1, blocking collectives, local(): lax.psum(jnp.concatenate([outer_side, inner_side], axis=1), 'tensor')  4.18 us
    dot_general x3, matrix products, contract_last(): lax.dot_general(left, right, (((1,), (1,)), ((), ())), preferred_element_...  3.85 us
  transfers between devices with their start and end apart: 1, of which 1 were waited for; matrix products, arithmetic and copies ran while one was open for 0% of the time, Pallas kernels for 0%

commit v1 on v0

v1 whole, which is shorter than its diff:
```python
import functools

import jax
import jax.numpy as jnp
from jax import lax
from jax.experimental import pallas as pl
from jax.experimental.pallas import tpu as pltpu
from jax.sharding import PartitionSpec as P


VMEM = pl.BlockSpec(memory_space=pltpu.VMEM)
LANES = 128


def dot_last(left, right):
    return lax.dot_general(
        left, right, (((1,), (1,)), ((), ())), preferred_element_type=jnp.float32
    )


def project_kernel(acts, grads, p_in, p_out, mask, out):
    rank = p_out.shape[1]
    keep = mask[...].astype(jnp.float32)
    out[:rank] = dot_last(p_out[0], grads[0]) * keep
    out[rank:] = dot_last(p_in[0], acts[0])


def project(acts, grads, p_in, p_out, mask):
    ranks = p_out.shape[1] + p_in.shape[1]
    toks = acts.shape[1]
    depth = acts.shape[2] + grads.shape[2]
    return pl.pallas_call(
        project_kernel,
        out_shape=jax.ShapeDtypeStruct((ranks, toks), jnp.float32),
        in_specs=[VMEM] * 5,
        out_specs=VMEM,
        compiler_params=pltpu.CompilerParams(vmem_limit_bytes=16 << 20),
        cost_estimate=pl.CostEstimate(
            flops=toks * ranks * depth,
            bytes_accessed=2 * depth * (toks + ranks // 2),
            transcendentals=0,
        ),
    )(acts, grads, p_in, p_out, mask)


def score_kernel(blocks, rank_out, pieces, *refs):
    sides, (bounds,), queries = refs[:blocks], refs[blocks : blocks + 1], refs[blocks + 1 : -1]
    out = refs[-1]
    toks = sides[0].shape[1]
    rows = bounds.shape[0]
    rank_in = sides[0].shape[0] - rank_out
    copies = LANES // rank_in
    lane = lax.broadcasted_iota(jnp.int32, (rows, toks), 1)
    total = None
    for c in range(blocks):
        inside = (lane >= bounds[:, 2 * c : 2 * c + 1]) & (lane < bounds[:, 2 * c + 1 : 2 * c + 2])
        g = sides[c][:rank_out].astype(jnp.float32)
        a = sides[c][rank_out:]
        spread = [jnp.where(inside, g[i : i + 1], 0.0) for i in range(rank_out)]
        weighted = jnp.concatenate(spread, axis=0).astype(jnp.bfloat16)
        part = dot_last(weighted, jnp.concatenate([a] * copies, axis=0))
        total = part if total is None else total + part
    column = lax.broadcasted_iota(jnp.int32, (rows, LANES), 1) // rank_in
    flat = []
    for i in range(0, rank_out, copies):
        tile = total[i * rows : (i + 1) * rows]
        for n in range(1, copies):
            tile = jnp.where(column == n, total[(i + n) * rows : (i + n + 1) * rows], tile)
        flat.append(tile)
    sketch = jnp.concatenate(flat, axis=1).astype(jnp.bfloat16)
    core = bounds[:, 2 * blocks : 2 * blocks + 1]
    place = bounds[:, 2 * blocks + 1 : 2 * blocks + 2]
    got = [dot_last(sketch, q[0] if len(q.shape) == 3 else q[...]) for q in queries]
    groups, at = [got[0]], 1
    for _ in range(1, pieces[0]):
        parts = got[at : at + pieces[1]]
        at += pieces[1]
        ordered = []
        for n in range(pieces[1]):
            pick = parts[0]
            for h in range(1, pieces[1]):
                pick = jnp.where((core ^ h) == n, parts[h], pick)
            if pieces[1] > 1:
                pick = jnp.where(core == n, parts[0], pick)
            ordered.append(pick)
        groups.append(jnp.concatenate(ordered, axis=1))
    final = []
    for n in range(pieces[0]):
        pick = groups[0]
        for h in range(1, pieces[0]):
            pick = jnp.where((place ^ h) == n, groups[h], pick)
        final.append(pick)
    out[...] = jnp.concatenate(final, axis=1)


def scores_of(sides, bounds, queries, rank_out, pieces):
    rows = bounds.shape[0]
    width = sum(q.shape[-2] for q in queries)
    depth = queries[0].shape[-1]
    return pl.pallas_call(
        functools.partial(score_kernel, len(sides), rank_out, pieces),
        out_shape=jax.ShapeDtypeStruct((rows, width), jnp.float32),
        in_specs=[VMEM] * (len(sides) + 1 + len(queries)),
        out_specs=VMEM,
        compiler_params=pltpu.CompilerParams(vmem_limit_bytes=24 << 20),
        cost_estimate=pl.CostEstimate(
            flops=2 * rows * depth * (width + len(sides) * sides[0].shape[1]),
            bytes_accessed=2 * depth * width,
            transcendentals=0,
        ),
    )(*sides, bounds, *queries)


def local(sizes, activations, out_grads, proj_in, proj_out, queries, lengths, owner_slot, pad_mask):
    dps, layers, cores = sizes
    pair = dps // layers
    toks = activations.shape[1]
    rank_out = proj_out.shape[1]
    block = queries.shape[1]
    own_rows = lengths.shape[0] // dps
    d, l, t = lax.axis_index("dp"), lax.axis_index("layer"), lax.axis_index("tensor")
    v = d % pair

    share = block // cores
    mine = lax.dynamic_slice_in_dim(queries[0], t * share, share, 0)
    fetched = []
    for k in range(1, pair):
        fetched.append(lax.ppermute(mine, "dp", [(i, i ^ k) for i in range(dps)]))

    partial_sides = project(activations, out_grads, proj_in, proj_out, pad_mask[None])
    both = partial_sides
    for k in range(1, cores):
        both = both + lax.ppermute(partial_sides, "tensor", [(i, i ^ k) for i in range(cores)])
    sides = both.astype(jnp.bfloat16)

    grouped, left = divmod(dps - 1, cores)
    held, source, split = [sides], [d], [True]
    for j in range(grouped - 1, -1, -1):
        base = 1 + left + j * cores
        perm = [
            (i * cores + c, (i ^ (base + cores - 1 - c)) * cores + c)
            for i in range(dps)
            for c in range(cores)
        ]
        held.append(lax.ppermute(sides, ("dp", "tensor"), perm))
        source.append(d ^ (base + cores - 1 - t))
        split.append(False)
    for k in range(left, 0, -1):
        held.append(lax.ppermute(sides, "dp", [(i, i ^ k) for i in range(dps)]))
        source.append(d ^ k)
        split.append(cores > 1)

    wanted = [queries]
    for q in fetched:
        wanted.append(q)
        for k in range(1, cores):
            wanted.append(lax.ppermute(q, "tensor", [(i, i ^ k) for i in range(cores)]))

    rows = layers * own_rows
    padded = -(-rows // 8) * 8
    index = jnp.arange(padded, dtype=jnp.int32)
    slot = ((l ^ (index // own_rows)) * pair + v) * own_rows + index % own_rows
    slot = jnp.where(index < rows, slot, -1)
    ones = jnp.arange(lengths.shape[0])
    first = jnp.sum(jnp.where(ones[None, :] < ones[:, None], lengths[None, :], 0), axis=1)
    match = slot[:, None] == owner_slot[None, :]
    low = jnp.sum(jnp.where(match, first[None, :], 0), axis=1)
    size = jnp.sum(jnp.where(match, lengths[None, :], 0), axis=1)
    columns = []
    for src, cut in zip(source, split):
        start = low - src * toks
        stop = start + size
        if cut:
            start = jnp.maximum(start, t * (toks // cores))
            stop = jnp.minimum(stop, (t + 1) * (toks // cores))
        columns += [start, stop]
    columns += [jnp.full_like(low, 1) * t, jnp.full_like(low, 1) * v]
    bounds = jnp.stack(columns, axis=1)

    served = scores_of(held, bounds, wanted, rank_out, (pair, cores))

    whole = None
    for k in range(layers - 1, -1, -1):
        turn = 1 if k == 0 else 0
        perm = []
        for su in range(layers):
            for sv in range(pair):
                for sl in range(layers):
                    for c in range(cores):
                        src = ((su * pair + sv) * layers + sl) * cores + c
                        dst = ((sl ^ k) * pair + sv) * layers + su
                        perm.append((src, dst * cores + (c + turn) % cores))
        piece = served[k * own_rows : (k + 1) * own_rows]
        piece = lax.ppermute(piece, ("dp", "layer", "tensor"), perm)
        whole = piece if whole is None else whole + piece
    result = whole
    for k in range(1, cores):
        result = result + lax.ppermute(whole, "tensor", [(i, i ^ k) for i in range(cores)])
    return result


def solution(mesh):
    placed = (
        P("layer", ("groups", "dp"), "tensor"),
        P("layer", ("groups", "dp"), "tensor"),
        P("layer", None, "tensor"),
        P("layer", None, "tensor"),
        P("layer", "dp", None),
        P("groups"),
        P("groups"),
        P(("groups", "dp")),
    )
    sizes = tuple(mesh.shape[name] for name in ("dp", "layer", "tensor"))
    return jax.shard_map(
        functools.partial(local, sizes),
        mesh=mesh,
        in_specs=placed,
        out_specs=P(("groups", "dp"), "layer"),
        check_vma=False,
    )
```

time: 67.4 us -> 32.8 us (0.49)
  blocking collectives: 34.7 us -> 0 us
  between operations: 13.5 us -> 0.07 us
  starting transfers between devices: 0.04 us -> 10.2 us
  waiting for transfers between devices: 8.74 us -> 12.8 us
  matrix products: 4.06 us -> 0 us
  Pallas kernels: 0 us -> 2.43 us
  local copies, waits for them, and re-layouts: 4.9 us -> 6.19 us
    psum x2 -> x0, blocking collectives: 26.8 us -> none  [the longest x1 22.7 us: local(): everyone = lax.psum(partial_value, 'dp').astype(jnp.bfloat16)]
    ppermute x0 -> x8, waiting for transfers between devices: none -> 12.8 us  [the longest x1 6.27 us: local(): fetched.append(lax.ppermute(mine, 'dp', [(i, i ^ k) for i in range(dps)]))]
    ppermute x0 -> x8, starting transfers between devices: none -> 10.2 us  [the longest x1 2.67 us: local(): fetched.append(lax.ppermute(mine, 'dp', [(i, i ^ k) for i in range(dps)]))]
    unnamed x2 -> x0, waiting for transfers between devices: 8.74 us -> none
    all_to_all x1 -> x0, blocking collectives: 7.91 us -> none  [spread_scores(): lax.all_to_all(local_scores, 'dp', split_axis=0, concat_axis=1, tiled=True)]
    dot_general x4 -> x0, matrix products: 4.06 us -> none  [the longest x3 3.85 us: contract_last(): lax.dot_general(left, right, (((1,), (1,)), ((), ())), preferred_element_...]
    pallas_call x0 -> x2, Pallas kernels: none -> 2.43 us  [the longest x1 1.24 us: project(): pl.pallas_call(project_kernel, out_shape=jax.ShapeDtypeStruct((ranks, tok...]
    unnamed x16, local copies, waits for them, and re-layouts: 4.21 us -> 5.75 us
  transfers between devices with their start and end apart: 1 -> 8, of which waited for: 1 -> 5; matrix products, arithmetic and copies ran while one was open for 0% -> 2% of each run, Pallas kernels for 0% -> 0%
where the time goes in v1:
time: 32.8 us; the launch traced here: 32.5 us
  waiting for transfers between devices  12.8 us (39%)
  starting transfers between devices  10.2 us (31%)
  local copies, waits for them, and re-layouts  6.19 us (19%)
  Pallas kernels  2.43 us (7%)
  other arithmetic  0.9 us (3%)
    ppermute x1, waiting for transfers between devices, local(): fetched.append(lax.ppermute(mine, 'dp', [(i, i ^ k) for i in range(dps)]))  6.27 us
    unnamed x16, local copies, waits for them, and re-layouts  5.75 us
    ppermute x1, waiting for transfers between devices, local(): held.append(lax.ppermute(sides, ('dp', 'tensor'), perm))  3.69 us
    ppermute x1, starting transfers between devices, local(): fetched.append(lax.ppermute(mine, 'dp', [(i, i ^ k) for i in range(dps)]))  2.67 us
    ppermute x1, starting transfers between devices, local(): held.append(lax.ppermute(sides, ('dp', 'tensor'), perm))  2.47 us
    ppermute x2, starting transfers between devices, local(): piece = lax.ppermute(piece, ('dp', 'layer', 'tensor'), perm)  1.86 us
    ppermute x1, starting transfers between devices, local(): held.append(lax.ppermute(sides, 'dp', [(i, i ^ k) for i in range(dps)]))  1.81 us
    ppermute x2, waiting for transfers between devices, local(): piece = lax.ppermute(piece, ('dp', 'layer', 'tensor'), perm)  1.77 us
  transfers between devices with their start and end apart: 8, of which 5 were waited for; matrix products, arithmetic and copies ran while one was open for 2% of the time, Pallas kernels for 0%

profile of v1, /device:TPU:0, one launch (start us, length us, event | category | flops | bytes accessed | tf_op | source)
XLA Modules:
  0.0 32.5 jit_solution(6329123663472903887)
XLA Ops:
  0.0 0.0 copy-start.6
  0.0 0.0 copy-start.7
  0.0 0.0 copy-start
  0.0 1.8 %copy-done = bf16[1,192,7168]{2,1,0:T(8,128)(2,1)S(1)} copy-done((bf16[1,192,7168]{2,1,0:T(8,128)(2,1)S(1)}, bf16[1,192,7168]{2,1,0:T(8,128)(2,1)}, u32[]{:S(2)}) %copy-start) | copy-done | bytes 2752536
  1.8 0.0 copy-start.2
  1.8 1.2 %copy-done.2 = bf16[1,64,7168]{2,1,0:T(8,128)(2,1)S(1)} copy-done((bf16[1,64,7168]{2,1,0:T(8,128)(2,1)S(1)}, bf16[1,64,7168]{2,1,0:T(8,128)(2,1)}, u32[]{:S(2)}) %copy-start.2) | copy-done | bytes 917528
  3.0 0.0 copy-start.3
  3.0 1.1 %copy-done.3 = bf16[1,192,2048]{2,1,0:T(8,128)(2,1)S(1)} copy-done((bf16[1,192,2048]{2,1,0:T(8,128)(2,1)S(1)}, bf16[1,192,2048]{2,1,0:T(8,128)(2,1)}, u32[]{:S(2)}) %copy-start.3) | copy-done | bytes 786456
  4.1 0.0 copy-start.4
  4.1 0.9 %copy-done.4 = bf16[1,64,2048]{2,1,0:T(8,128)(2,1)S(1)} copy-done((bf16[1,64,2048]{2,1,0:T(8,128)(2,1)S(1)}, bf16[1,64,2048]{2,1,0:T(8,128)(2,1)}, u32[]{:S(2)}) %copy-start.4) | copy-done | bytes 262168
  5.1 0.0 copy-start.5
  5.1 0.7 %copy-done.5 = s32[192]{0:T(256)S(1)} copy-done((s32[192]{0:T(256)S(1)}, s32[192]{0:T(256)}, u32[]{:S(2)}) %copy-start.5) | copy-done | bytes 792
  5.8 0.0 copy-start.1
  5.8 1.2 %shard_map.82 = f32[128,192]{1,0:T(8,128)S(1)} custom-call(bf16[1,192,7168]{2,1,0:T(8,128)(2,1)S(1)} %copy-done, bf16[1,192,2048]{2,1,0:T(8,128)(2,1)S(1)} %copy-done.3, bf16[1,64,7168]{2,1,0:T(8,128)(2,1)S(1)} %copy-done.2, bf16[1,64,2048]{2,1,0:T(8,128)(2,1)S(1)} %copy-done.4, s32[1,192]{1,0:T(1,128)S(1)} %bitcast.10), custom_call_target="tpu_custom_call" | custom-call | flops 226492416 | bytes 4718592 | tf_op jit(solution)/shard_map/pallas_call | solution.py:32
  7.0 0.6 %collective-permute-start = (f32[128,192]{1,0:T(8,128)S(1)}, f32[128,192]{1,0:T(8,128)S(1)}, u32[]{:S(2)}, u32[]{:S(2)}) collective-permute-start(f32[128,192]{1,0:T(8,128)S(1)} %shard_map.82), channel_id=1, source_target_pairs={{0,1},{1,0},{2,3},{3,2},{4,5},{5,4},{6,7},{7,6},{8,9},{9,8},{10,11... | collective-permute-start | bytes 294920 | tf_op jit(solution)/shard_map/ppermute | solution.py:133
  7.5 0.0 copy-done.1
  7.6 2.7 %collective-permute-start.3 = (bf16[32,4096]{1,0:T(8,128)(2,1)S(1)}, bf16[32,4096]{1,0:T(8,128)(2,1)S(1)}, u32[]{:S(2)}, u32[]{:S(2)}) collective-permute-start(bf16[32,4096]{1,0:T(8,128)(2,1)S(1)} %dynamic-slice_bitcast_fusion), channel_id=1, source_target_pairs={{0,4},{4,0},{8,12},{12,8},{1,5},{5,1},{9,13},{13,9},{2,6},{6,2},{1... | collective-permute-start | bytes 786440 | tf_op jit(solution)/shard_map/ppermute | solution.py:128
  10.2 0.0 copy-done.6
  10.2 0.1 select_reduce_fusion
  10.4 0.0 copy-done.7
  10.4 0.2 fusion.1
  10.6 0.1 copy.23
  10.7 0.1 copy.20
  10.8 0.1 copy.26
  10.8 0.1 copy.18
  10.9 6.3 %collective-permute-done.3.refs_5_ = bf16[32,4096]{1,0:T(8,128)(2,1)S(1)} collective-permute-done((bf16[32,4096]{1,0:T(8,128)(2,1)S(1)}, bf16[32,4096]{1,0:T(8,128)(2,1)S(1)}, u32[]{:S(2)}, u32[]{:S(2)}) %collective-permute-start.3) | collective-permute-done | bytes 262176 | tf_op jit(solution)/shard_map/ppermute | solution.py:128
  17.2 0.0 collective-permute-start.4
  17.2 0.0 collective-permute-done
  17.2 1.8 %collective-permute-start.2 = (bf16[128,192]{1,0:T(8,128)(2,1)S(1)}, bf16[128,192]{1,0:T(8,128)(2,1)S(1)}, u32[]{:S(2)}, u32[]{:S(2)}) collective-permute-start(bf16[128,192]{1,0:T(8,128)(2,1)S(1)} %add_convert_fusion.refs_0_), channel_id=1, source_target_pairs={{0,4},{4,0},{8,12},{12,8},{1,5},{5,1},{9,13},{13,9},{2,6},{6,2},{1... | collective-permute-start | bytes 147464 | tf_op jit(solution)/shard_map/ppermute | solution.py:149
  19.0 2.5 %collective-permute-start.1 = (bf16[128,192]{1,0:T(8,128)(2,1)S(1)}, bf16[128,192]{1,0:T(8,128)(2,1)S(1)}, u32[]{:S(2)}, u32[]{:S(2)}) collective-permute-start(bf16[128,192]{1,0:T(8,128)(2,1)S(1)} %add_convert_fusion.refs_0_), channel_id=1, source_target_pairs={{0,12},{1,9},{4,8},{5,13},{8,4},{9,1},{12,0},{13,5},{2,14},{3,11},... | collective-permute-start | bytes 147464 | tf_op jit(solution)/shard_map/ppermute | solution.py:145
  21.5 0.1 stack.5.refs_3_
  21.6 0.2 collective-permute-done.2.refs_2_
  21.8 3.7 %collective-permute-done.1.refs_1_ = bf16[128,192]{1,0:T(8,128)(2,1)S(1)} collective-permute-done((bf16[128,192]{1,0:T(8,128)(2,1)S(1)}, bf16[128,192]{1,0:T(8,128)(2,1)S(1)}, u32[]{:S(2)}, u32[]{:S(2)}) %collective-permute-start.1) | collective-permute-done | bytes 49184 | tf_op jit(solution)/shard_map/ppermute | solution.py:145
  25.5 0.0 collective-permute-done.4.refs_6_
  25.5 1.2 %shard_map.83 = f32[8,128]{1,0:T(8,128)S(1)} custom-call(bf16[128,192]{1,0:T(8,128)(2,1)S(1)} %add_convert_fusion.refs_0_, bf16[128,192]{1,0:T(8,128)(2,1)S(1)} %collective-permute-done.1.refs_1_, bf16[128,192]{1,0:T(8,128)(2,1)S(1)} %collective-permute-done.2.refs_2_, s32[8,8]{1,0:T(8,128)S(1)} %stack.5.refs_3_, bf16[1,64,4096]{2,1,0:T(8,128)(2,1)S(1)} %copy-done.1, ...), custom_call_target="tpu_custom_call" | custom-call | flops 46137344 | bytes 1048576 | tf_op jit(solution)/shard_map/pallas_call | solution.py:100
  26.7 0.0 collective-permute-start.6
  26.7 1.9 %collective-permute-start.5 = (f32[2,128]{1,0:T(2,128)S(1)}, f32[2,128]{1,0:T(2,128)S(1)}, u32[]{:S(2)}, u32[]{:S(2)}) collective-permute-start(f32[2,128]{1,0:T(2,128)S(1)} %get-tuple-element.8), channel_id=1, source_target_pairs={{0,8},{1,9},{2,0},{3,1},{4,12},{5,13},{6,4},{7,5},{8,10},{9,11},{1... | collective-permute-start | bytes 3080 | tf_op jit(solution)/shard_map/ppermute | solution.py:194
  28.5 0.0 collective-permute-done.6
  28.5 1.8 %collective-permute-done.5 = f32[2,128]{1,0:T(2,128)S(1)} collective-permute-done((f32[2,128]{1,0:T(2,128)S(1)}, f32[2,128]{1,0:T(2,128)S(1)}, u32[]{:S(2)}, u32[]{:S(2)}) %collective-permute-start.5) | collective-permute-done | bytes 1056 | tf_op jit(solution)/shard_map/ppermute | solution.py:194
  30.3 0.8 %collective-permute-start.7 = (f32[2,128]{1,0:T(2,128)S(1)}, f32[2,128]{1,0:T(2,128)S(1)}, u32[]{:S(2)}, u32[]{:S(2)}) collective-permute-start(f32[2,128]{1,0:T(2,128)S(1)} %add.96), channel_id=1, source_target_pairs={{0,1},{1,0},{2,3},{3,2},{4,5},{5,4},{6,7},{7,6},{8,9},{9,8},{10,11... | collective-permute-start | bytes 3080 | tf_op jit(solution)/shard_map/ppermute | solution.py:198
  31.1 0.8 %collective-permute-done.7 = f32[2,128]{1,0:T(2,128)S(1)} collective-permute-done((f32[2,128]{1,0:T(2,128)S(1)}, f32[2,128]{1,0:T(2,128)S(1)}, u32[]{:S(2)}, u32[]{:S(2)}) %collective-permute-start.7) | collective-permute-done | bytes 1056 | tf_op jit(solution)/shard_map/ppermute | solution.py:198
  31.9 0.6 %add.97 = f32[2,128]{1,0:T(2,128)} add(f32[2,128]{1,0:T(2,128)S(1)} %add.96, f32[2,128]{1,0:T(2,128)S(1)} %collective-permute-done.7) | non-fusion elementwise | flops 256 | bytes 3072 | tf_op jit(solution)/shard_map/add | solution.py:198
  (9 shorter events, 0.1 us)
Async XLA Ops:
  0.0 10.2 %copy-start.6 = (s32[8]{0:T(128)S(1)}, s32[8]{0:T(128)}, u32[]{:S(2)}) copy-start(s32[8]{0:T(128)} %param.13) | copy-start | bytes 100
  0.0 10.4 %copy-start.7 = (s32[8]{0:T(128)S(1)}, s32[8]{0:T(128)}, u32[]{:S(2)}) copy-start(s32[8]{0:T(128)} %param.14) | copy-start | bytes 100
  0.0 1.8 %copy-start = (bf16[1,192,7168]{2,1,0:T(8,128)(2,1)S(1)}, bf16[1,192,7168]{2,1,0:T(8,128)(2,1)}, u32[]{:S(2)}) copy-start(bf16[1,192,7168]{2,1,0:T(8,128)(2,1)} %acts.1) | copy-start | bytes 8257540
  1.8 1.2 %copy-start.2 = (bf16[1,64,7168]{2,1,0:T(8,128)(2,1)S(1)}, bf16[1,64,7168]{2,1,0:T(8,128)(2,1)}, u32[]{:S(2)}) copy-start(bf16[1,64,7168]{2,1,0:T(8,128)(2,1)} %p_in.1) | copy-start | bytes 2752516
  3.0 1.1 %copy-start.3 = (bf16[1,192,2048]{2,1,0:T(8,128)(2,1)S(1)}, bf16[1,192,2048]{2,1,0:T(8,128)(2,1)}, u32[]{:S(2)}) copy-start(bf16[1,192,2048]{2,1,0:T(8,128)(2,1)} %grads.1) | copy-start | bytes 2359300
  4.1 0.9 %copy-start.4 = (bf16[1,64,2048]{2,1,0:T(8,128)(2,1)S(1)}, bf16[1,64,2048]{2,1,0:T(8,128)(2,1)}, u32[]{:S(2)}) copy-start(bf16[1,64,2048]{2,1,0:T(8,128)(2,1)} %p_out.1) | copy-start | bytes 786436
  5.1 0.7 %copy-start.5 = (s32[192]{0:T(256)S(1)}, s32[192]{0:T(256)}, u32[]{:S(2)}) copy-start(s32[192]{0:T(256)} %param.15) | copy-start | bytes 2308
  5.8 1.8 %copy-start.1 = (bf16[1,64,4096]{2,1,0:T(8,128)(2,1)S(1)}, bf16[1,64,4096]{2,1,0:T(8,128)(2,1)}, u32[]{:S(2)}) copy-start(bf16[1,64,4096]{2,1,0:T(8,128)(2,1)} %refs_4_.1) | copy-start | bytes 1572868
  7.0 10.2 %collective-permute-start = (f32[128,192]{1,0:T(8,128)S(1)}, f32[128,192]{1,0:T(8,128)S(1)}, u32[]{:S(2)}, u32[]{:S(2)}) collective-permute-start(f32[128,192]{1,0:T(8,128)S(1)} %shard_map.82), channel_id=1, source_target_pairs={{0,1},{1,0},{2,3},{3,2},{4,5},{5,4},{6,7},{7,6},{8,9},{9,8},{10,11... | collective-permute-start | bytes 294920 | tf_op jit(solution)/shard_map/ppermute | solution.py:133
  7.6 9.6 %collective-permute-start.3 = (bf16[32,4096]{1,0:T(8,128)(2,1)S(1)}, bf16[32,4096]{1,0:T(8,128)(2,1)S(1)}, u32[]{:S(2)}, u32[]{:S(2)}) collective-permute-start(bf16[32,4096]{1,0:T(8,128)(2,1)S(1)} %dynamic-slice_bitcast_fusion), channel_id=1, source_target_pairs={{0,4},{4,0},{8,12},{12,8},{1,5},{5,1},{9,13},{13,9},{2,6},{6,2},{1... | collective-permute-start | bytes 786440 | tf_op jit(solution)/shard_map/ppermute | solution.py:128
  17.2 8.3 %collective-permute-start.4 = (bf16[32,4096]{1,0:T(8,128)(2,1)S(1)}, bf16[32,4096]{1,0:T(8,128)(2,1)S(1)}, u32[]{:S(2)}, u32[]{:S(2)}) collective-permute-start(bf16[32,4096]{1,0:T(8,128)(2,1)S(1)} %collective-permute-done.3.refs_5_), channel_id=1, source_target_pairs={{0,1},{1,0},{2,3},{3,2},{4,5},{5,4},{6,7},{7,6},{8,9},{9,8},{10,11... | collective-permute-start | bytes 786440 | tf_op jit(solution)/shard_map/ppermute | solution.py:157
  17.2 4.6 %collective-permute-start.2 = (bf16[128,192]{1,0:T(8,128)(2,1)S(1)}, bf16[128,192]{1,0:T(8,128)(2,1)S(1)}, u32[]{:S(2)}, u32[]{:S(2)}) collective-permute-start(bf16[128,192]{1,0:T(8,128)(2,1)S(1)} %add_convert_fusion.refs_0_), channel_id=1, source_target_pairs={{0,4},{4,0},{8,12},{12,8},{1,5},{5,1},{9,13},{13,9},{2,6},{6,2},{1... | collective-permute-start | bytes 147464 | tf_op jit(solution)/shard_map/ppermute | solution.py:149
  19.0 6.5 %collective-permute-start.1 = (bf16[128,192]{1,0:T(8,128)(2,1)S(1)}, bf16[128,192]{1,0:T(8,128)(2,1)S(1)}, u32[]{:S(2)}, u32[]{:S(2)}) collective-permute-start(bf16[128,192]{1,0:T(8,128)(2,1)S(1)} %add_convert_fusion.refs_0_), channel_id=1, source_target_pairs={{0,12},{1,9},{4,8},{5,13},{8,4},{9,1},{12,0},{13,5},{2,14},{3,11},... | collective-permute-start | bytes 147464 | tf_op jit(solution)/shard_map/ppermute | solution.py:145
  26.7 1.9 %collective-permute-start.6 = (f32[2,128]{1,0:T(2,128)S(1)}, f32[2,128]{1,0:T(2,128)S(1)}, u32[]{:S(2)}, u32[]{:S(2)}) collective-permute-start(f32[2,128]{1,0:T(2,128)S(1)} %get-tuple-element.7), channel_id=1, source_target_pairs={{0,1},{1,0},{2,9},{3,8},{4,5},{5,4},{6,13},{7,12},{8,3},{9,2},{10,... | collective-permute-start | bytes 3080 | tf_op jit(solution)/shard_map/ppermute | solution.py:194
  26.7 3.6 %collective-permute-start.5 = (f32[2,128]{1,0:T(2,128)S(1)}, f32[2,128]{1,0:T(2,128)S(1)}, u32[]{:S(2)}, u32[]{:S(2)}) collective-permute-start(f32[2,128]{1,0:T(2,128)S(1)} %get-tuple-element.8), channel_id=1, source_target_pairs={{0,8},{1,9},{2,0},{3,1},{4,12},{5,13},{6,4},{7,5},{8,10},{9,11},{1... | collective-permute-start | bytes 3080 | tf_op jit(solution)/shard_map/ppermute | solution.py:194
  30.3 1.6 %collective-permute-start.7 = (f32[2,128]{1,0:T(2,128)S(1)}, f32[2,128]{1,0:T(2,128)S(1)}, u32[]{:S(2)}, u32[]{:S(2)}) collective-permute-start(f32[2,128]{1,0:T(2,128)S(1)} %add.96), channel_id=1, source_target_pairs={{0,1},{1,0},{2,3},{3,2},{4,5},{5,4},{6,7},{7,6},{8,9},{9,8},{10,11... | collective-permute-start | bytes 3080 | tf_op jit(solution)/shard_map/ppermute | solution.py:198

commit v2 on v1

--- a/solution.py
+++ b/solution.py
@@ -10,6 +10,7 @@
 
 VMEM = pl.BlockSpec(memory_space=pltpu.VMEM)
 LANES = 128
+CHUNKS = 4
 
 
 def dot_last(left, right):
@@ -18,29 +19,56 @@
     )
 
 
-def project_kernel(acts, grads, p_in, p_out, mask, out):
+def cuts(depth, count):
+    step = max(LANES, depth // count // LANES * LANES)
+    edges = list(range(0, depth - step + 1, step))
+    return [(lo, (edges + [depth])[n + 1] - lo) for n, lo in enumerate(edges)]
+
+
+def project_kernel(acts, grads, p_in, p_out, out, acts_v, grads_v, in_v, out_v, sems):
     rank = p_out.shape[1]
-    keep = mask[...].astype(jnp.float32)
-    out[:rank] = dot_last(p_out[0], grads[0]) * keep
-    out[rank:] = dot_last(p_in[0], acts[0])
-
-
-def project(acts, grads, p_in, p_out, mask):
+    chunks = cuts(acts.shape[2], CHUNKS)
+    waits = []
+    for n, (lo, size) in enumerate([(0, grads.shape[2])] + chunks):
+        pairs = [(grads, grads_v), (p_out, out_v)] if n == 0 else [(acts, acts_v), (p_in, in_v)]
+        started = []
+        for m, (src, dst) in enumerate(pairs):
+            part = (slice(None), pl.ds(lo, size))
+            copy = pltpu.make_async_copy(src.at[(0,) + part], dst.at[part], sems.at[2 * n + m])
+            copy.start()
+            started.append(copy)
+        waits.append(started)
+    for copy in waits[0]:
+        copy.wait()
+    out[:rank] = dot_last(out_v[...], grads_v[...])
+    total = None
+    for (lo, size), started in zip(chunks, waits[1:]):
+        for copy in started:
+            copy.wait()
+        part = dot_last(in_v[:, pl.ds(lo, size)], acts_v[:, pl.ds(lo, size)])
+        total = part if total is None else total + part
+    out[rank:] = total
+
+
+def project(acts, grads, p_in, p_out):
     ranks = p_out.shape[1] + p_in.shape[1]
     toks = acts.shape[1]
     depth = acts.shape[2] + grads.shape[2]
+    big = [pltpu.with_memory_space_constraint(x, pltpu.HBM) for x in (acts, grads, p_in, p_out)]
     return pl.pallas_call(
         project_kernel,
         out_shape=jax.ShapeDtypeStruct((ranks, toks), jnp.float32),
-        in_specs=[VMEM] * 5,
+        in_specs=[pl.BlockSpec(memory_space=pltpu.HBM)] * 4,
         out_specs=VMEM,
+        scratch_shapes=[pltpu.VMEM(x.shape[1:], x.dtype) for x in big]
+        + [pltpu.SemaphoreType.DMA((2 * len(cuts(acts.shape[2], CHUNKS)) + 2,))],
         compiler_params=pltpu.CompilerParams(vmem_limit_bytes=16 << 20),
         cost_estimate=pl.CostEstimate(
             flops=toks * ranks * depth,
             bytes_accessed=2 * depth * (toks + ranks // 2),
             transcendentals=0,
         ),
-    )(acts, grads, p_in, p_out, mask)
+    )(*big)
 
 
 def score_kernel(blocks, rank_out, pieces, *refs):
@@ -75,15 +103,10 @@
     for _ in range(1, pieces[0]):
         parts = got[at : at + pieces[1]]
         at += pieces[1]
-        ordered = []
-        for n in range(pieces[1]):
-            pick = parts[0]
-            for h in range(1, pieces[1]):
-                pick = jnp.where((core ^ h) == n, parts[h], pick)
-            if pieces[1] > 1:
-                pick = jnp.where(core == n, parts[0], pick)
-            ordered.append(pick)
-        groups.append(jnp.concatenate(ordered, axis=1))
+        pick = parts[0]
+        for h in range(1, pieces[1]):
+            pick = jnp.where(core == (pieces[1] - 1 + h) % pieces[1], parts[h], pick)
+        groups.append(pick)
     final = []
     for n in range(pieces[0]):
         pick = groups[0]
@@ -95,7 +118,7 @@
 
 def scores_of(sides, bounds, queries, rank_out, pieces):
     rows = bounds.shape[0]
-    width = sum(q.shape[-2] for q in queries)
+    width = pieces[0] * queries[0].shape[-2]
     depth = queries[0].shape[-1]
     return pl.pallas_call(
         functools.partial(score_kernel, len(sides), rank_out, pieces),
@@ -116,22 +139,25 @@
     pair = dps // layers
     toks = activations.shape[1]
     rank_out = proj_out.shape[1]
-    block = queries.shape[1]
     own_rows = lengths.shape[0] // dps
     d, l, t = lax.axis_index("dp"), lax.axis_index("layer"), lax.axis_index("tensor")
     v = d % pair
 
-    share = block // cores
-    mine = lax.dynamic_slice_in_dim(queries[0], t * share, share, 0)
     fetched = []
     for k in range(1, pair):
-        fetched.append(lax.ppermute(mine, "dp", [(i, i ^ k) for i in range(dps)]))
-
-    partial_sides = project(activations, out_grads, proj_in, proj_out, pad_mask[None])
+        perm = [
+            (i * cores + c, (i if c else i ^ k) * cores + (c + cores - 1) % cores)
+            for i in range(dps)
+            for c in range(cores)
+        ]
+        fetched.append(lax.ppermute(queries[0], ("dp", "tensor"), perm))
+
+    partial_sides = project(activations, out_grads, proj_in, proj_out)
     both = partial_sides
     for k in range(1, cores):
         both = both + lax.ppermute(partial_sides, "tensor", [(i, i ^ k) for i in range(cores)])
-    sides = both.astype(jnp.bfloat16)
+    is_out = lax.broadcasted_iota(jnp.int32, both.shape, 0) < rank_out
+    sides = jnp.where(is_out & (pad_mask == 0)[None], 0.0, both).astype(jnp.bfloat16)
 
     grouped, left = divmod(dps - 1, cores)
     held, source, split = [sides], [d], [True]
@@ -154,7 +180,8 @@
     for q in fetched:
         wanted.append(q)
         for k in range(1, cores):
-            wanted.append(lax.ppermute(q, "tensor", [(i, i ^ k) for i in range(cores)]))
+            perm = [(i, (i + k) % cores) for i in range(cores)]
+            wanted.append(lax.ppermute(q, "tensor", perm))
 
     rows = layers * own_rows
     padded = -(-rows // 8) * 8

time: 32.8 us -> 29 us (0.88)
  local copies, waits for them, and re-layouts: 6.19 us -> 0.43 us
  Pallas kernels: 2.43 us -> 4.56 us
  waiting for transfers between devices: 12.8 us -> 12.1 us
  starting transfers between devices: 10.2 us -> 10.8 us
    unnamed x16 -> x8, local copies, waits for them, and re-layouts: 5.75 us -> 0.01 us
    pallas_call x1, Pallas kernels: 1.24 us -> 3.45 us  [project(): pl.pallas_call(project_kernel, out_shape=jax.ShapeDtypeStruct((ranks, tok...]
  transfers between devices with their start and end apart: 8 -> 8, of which waited for: 5 -> 4; matrix products, arithmetic and copies ran while one was open for 2% -> 3% of each run, Pallas kernels for 0% -> 0%
where the time goes in v2:
time: 29 us; the launch traced here: 28.9 us
  waiting for transfers between devices  12.1 us (42%)
  starting transfers between devices  10.8 us (37%)
  Pallas kernels  4.56 us (16%)
  other arithmetic  0.99 us (3%)
  local copies, waits for them, and re-layouts  0.43 us (1%)
    ppermute x1, waiting for transfers between devices, local(): fetched.append(lax.ppermute(queries[0], ('dp', 'tensor'), perm))  6.03 us
    ppermute x1, waiting for transfers between devices, local(): held.append(lax.ppermute(sides, ('dp', 'tensor'), perm))  3.49 us
    pallas_call x1, Pallas kernels, project(): pl.pallas_call(project_kernel, out_shape=jax.ShapeDtypeStruct((ranks, tok...  3.45 us
    ppermute x1, starting transfers between devices, local(): fetched.append(lax.ppermute(queries[0], ('dp', 'tensor'), perm))  2.67 us
    ppermute x1, starting transfers between devices, local(): held.append(lax.ppermute(sides, ('dp', 'tensor'), perm))  2.48 us
    ppermute x1, starting transfers between devices, local(): held.append(lax.ppermute(sides, 'dp', [(i, i ^ k) for i in range(dps)]))  2.13 us
    ppermute x2, starting transfers between devices, local(): piece = lax.ppermute(piece, ('dp', 'layer', 'tensor'), perm)  1.9 us
    ppermute x2, waiting for transfers between devices, local(): piece = lax.ppermute(piece, ('dp', 'layer', 'tensor'), perm)  1.72 us
  transfers between devices with their start and end apart: 8, of which 4 were waited for; matrix products, arithmetic and copies ran while one was open for 3% of the time, Pallas kernels for 0%

profile of v2, /device:TPU:0, one launch (start us, length us, event | category | flops | bytes accessed | tf_op | source)
XLA Modules:
  0.0 28.9 jit_solution(17147982025501682281)
XLA Ops:
  0.0 0.0 copy-start
  0.0 0.0 copy-start.1
  0.0 0.0 copy-start.2
  0.0 0.0 copy-start.3
  0.0 3.5 %shard_map.82 = f32[128,192]{1,0:T(8,128)S(1)} custom-call(bf16[1,192,7168]{2,1,0:T(8,128)(2,1)} %acts.1, bf16[1,192,2048]{2,1,0:T(8,128)(2,1)} %grads.1, bf16[1,64,7168]{2,1,0:T(8,128)(2,1)} %p_in.1, bf16[1,64,2048]{2,1,0:T(8,128)(2,1)} %p_out.1), custom_call_target="tpu_custom_call" | custom-call | flops 226492416 | bytes 4718592 | tf_op jit(solution)/shard_map/pallas_call | solution.py:58
  3.5 0.6 %collective-permute-start = (f32[128,192]{1,0:T(8,128)S(1)}, f32[128,192]{1,0:T(8,128)S(1)}, u32[]{:S(2)}, u32[]{:S(2)}) collective-permute-start(f32[128,192]{1,0:T(8,128)S(1)} %shard_map.82), channel_id=1, source_target_pairs={{0,1},{1,0},{2,3},{3,2},{4,5},{5,4},{6,7},{7,6},{8,9},{9,8},{10,11... | collective-permute-start | bytes 294920 | tf_op jit(solution)/shard_map/ppermute | solution.py:158
  4.0 0.0 copy-done
  4.0 2.7 %collective-permute-start.3 = (bf16[64,4096]{1,0:T(8,128)(2,1)S(1)}, bf16[64,4096]{1,0:T(8,128)(2,1)S(1)}, u32[]{:S(2)}, u32[]{:S(2)}) collective-permute-start(bf16[64,4096]{1,0:T(8,128)(2,1)S(1)} %bitcast.8), channel_id=1, source_target_pairs={{0,5},{1,0},{4,1},{5,4},{8,13},{9,8},{12,9},{13,12},{2,7},{3,2},{6... | collective-permute-start | bytes 1572872 | tf_op jit(solution)/shard_map/ppermute | solution.py:153
  6.7 0.0 copy-done.1
  6.7 0.1 select_reduce_fusion
  6.8 0.0 copy-done.2
  6.9 0.2 fusion.1
  7.1 0.1 copy.23
  7.1 0.1 copy.20
  7.2 0.1 copy.26
  7.3 0.1 copy.18
  7.4 0.0 copy-done.3
  7.4 6.0 %collective-permute-done.3.refs_5_ = bf16[64,4096]{1,0:T(8,128)(2,1)S(1)} collective-permute-done((bf16[64,4096]{1,0:T(8,128)(2,1)S(1)}, bf16[64,4096]{1,0:T(8,128)(2,1)S(1)}, u32[]{:S(2)}, u32[]{:S(2)}) %collective-permute-start.3) | collective-permute-done | bytes 524320 | tf_op jit(solution)/shard_map/ppermute | solution.py:153
  13.4 0.2 collective-permute-start.4
  13.7 0.0 collective-permute-done
  13.7 0.1 select_convert_fusion.refs_0_
  13.8 2.1 %collective-permute-start.2 = (bf16[128,192]{1,0:T(8,128)(2,1)S(1)}, bf16[128,192]{1,0:T(8,128)(2,1)S(1)}, u32[]{:S(2)}, u32[]{:S(2)}) collective-permute-start(bf16[128,192]{1,0:T(8,128)(2,1)S(1)} %select_convert_fusion.refs_0_), channel_id=1, source_target_pairs={{0,4},{4,0},{8,12},{12,8},{1,5},{5,1},{9,13},{13,9},{2,6},{6,2},{1... | collective-permute-start | bytes 147464 | tf_op jit(solution)/shard_map/ppermute | solution.py:175
  15.9 2.5 %collective-permute-start.1 = (bf16[128,192]{1,0:T(8,128)(2,1)S(1)}, bf16[128,192]{1,0:T(8,128)(2,1)S(1)}, u32[]{:S(2)}, u32[]{:S(2)}) collective-permute-start(bf16[128,192]{1,0:T(8,128)(2,1)S(1)} %select_convert_fusion.refs_0_), channel_id=1, source_target_pairs={{0,12},{1,9},{4,8},{5,13},{8,4},{9,1},{12,0},{13,5},{2,14},{3,11},... | collective-permute-start | bytes 147464 | tf_op jit(solution)/shard_map/ppermute | solution.py:171
  18.4 0.1 stack.5.refs_3_
  18.5 0.0 collective-permute-done.2.refs_2_
  18.5 3.5 %collective-permute-done.1.refs_1_ = bf16[128,192]{1,0:T(8,128)(2,1)S(1)} collective-permute-done((bf16[128,192]{1,0:T(8,128)(2,1)S(1)}, bf16[128,192]{1,0:T(8,128)(2,1)S(1)}, u32[]{:S(2)}, u32[]{:S(2)}) %collective-permute-start.1) | collective-permute-done | bytes 49184 | tf_op jit(solution)/shard_map/ppermute | solution.py:171
  21.9 0.0 collective-permute-done.4.refs_6_
  22.0 1.1 %shard_map.83 = f32[8,128]{1,0:T(8,128)S(1)} custom-call(bf16[128,192]{1,0:T(8,128)(2,1)S(1)} %select_convert_fusion.refs_0_, bf16[128,192]{1,0:T(8,128)(2,1)S(1)} %collective-permute-done.1.refs_1_, bf16[128,192]{1,0:T(8,128)(2,1)S(1)} %collective-permute-done.2.refs_2_, s32[8,8]{1,0:T(8,128)S(1)} %stack.5.refs_3_, bf16[1,64,4096]{2,1,0:T(8,128)(2,1)S(1)} %copy-done, ...), custom_call_target="tpu_custom_call" | custom-call | flops 46137344 | bytes 1048576 | tf_op jit(solution)/shard_map/pallas_call | solution.py:123
  23.1 0.0 collective-permute-start.6
  23.1 1.9 %collective-permute-start.5 = (f32[2,128]{1,0:T(2,128)S(1)}, f32[2,128]{1,0:T(2,128)S(1)}, u32[]{:S(2)}, u32[]{:S(2)}) collective-permute-start(f32[2,128]{1,0:T(2,128)S(1)} %get-tuple-element.8), channel_id=1, source_target_pairs={{0,8},{1,9},{2,0},{3,1},{4,12},{5,13},{6,4},{7,5},{8,10},{9,11},{1... | collective-permute-start | bytes 3080 | tf_op jit(solution)/shard_map/ppermute | solution.py:221
  25.0 0.0 collective-permute-done.6
  25.0 1.7 %collective-permute-done.5 = f32[2,128]{1,0:T(2,128)S(1)} collective-permute-done((f32[2,128]{1,0:T(2,128)S(1)}, f32[2,128]{1,0:T(2,128)S(1)}, u32[]{:S(2)}, u32[]{:S(2)}) %collective-permute-start.5) | collective-permute-done | bytes 1056 | tf_op jit(solution)/shard_map/ppermute | solution.py:221
  26.7 0.8 %collective-permute-start.7 = (f32[2,128]{1,0:T(2,128)S(1)}, f32[2,128]{1,0:T(2,128)S(1)}, u32[]{:S(2)}, u32[]{:S(2)}) collective-permute-start(f32[2,128]{1,0:T(2,128)S(1)} %add.92), channel_id=1, source_target_pairs={{0,1},{1,0},{2,3},{3,2},{4,5},{5,4},{6,7},{7,6},{8,9},{9,8},{10,11... | collective-permute-start | bytes 3080 | tf_op jit(solution)/shard_map/ppermute | solution.py:225
  27.5 0.8 %collective-permute-done.7 = f32[2,128]{1,0:T(2,128)S(1)} collective-permute-done((f32[2,128]{1,0:T(2,128)S(1)}, f32[2,128]{1,0:T(2,128)S(1)}, u32[]{:S(2)}, u32[]{:S(2)}) %collective-permute-start.7) | collective-permute-done | bytes 1056 | tf_op jit(solution)/shard_map/ppermute | solution.py:225
  28.3 0.6 %add.93 = f32[2,128]{1,0:T(2,128)} add(f32[2,128]{1,0:T(2,128)S(1)} %add.92, f32[2,128]{1,0:T(2,128)S(1)} %collective-permute-done.7) | non-fusion elementwise | flops 256 | bytes 3072 | tf_op jit(solution)/shard_map/add | solution.py:225
  (9 shorter events, 0.0 us)
Async XLA Ops:
  0.0 4.0 %copy-start = (bf16[1,64,4096]{2,1,0:T(8,128)(2,1)S(1)}, bf16[1,64,4096]{2,1,0:T(8,128)(2,1)}, u32[]{:S(2)}) copy-start(bf16[1,64,4096]{2,1,0:T(8,128)(2,1)} %refs_4_.1) | copy-start | bytes 1572868
  0.0 6.7 %copy-start.1 = (s32[8]{0:T(128)S(1)}, s32[8]{0:T(128)}, u32[]{:S(2)}) copy-start(s32[8]{0:T(128)} %param.13) | copy-start | bytes 100
  0.0 6.8 %copy-start.2 = (s32[8]{0:T(128)S(1)}, s32[8]{0:T(128)}, u32[]{:S(2)}) copy-start(s32[8]{0:T(128)} %param.14) | copy-start | bytes 100
  0.0 7.4 %copy-start.3 = (s32[192]{0:T(256)S(1)}, s32[192]{0:T(256)}, u32[]{:S(2)}) copy-start(s32[192]{0:T(256)} %param.15) | copy-start | bytes 2308
  3.5 10.2 %collective-permute-start = (f32[128,192]{1,0:T(8,128)S(1)}, f32[128,192]{1,0:T(8,128)S(1)}, u32[]{:S(2)}, u32[]{:S(2)}) collective-permute-start(f32[128,192]{1,0:T(8,128)S(1)} %shard_map.82), channel_id=1, source_target_pairs={{0,1},{1,0},{2,3},{3,2},{4,5},{5,4},{6,7},{7,6},{8,9},{9,8},{10,11... | collective-permute-start | bytes 294920 | tf_op jit(solution)/shard_map/ppermute | solution.py:158
  4.0 9.4 %collective-permute-start.3 = (bf16[64,4096]{1,0:T(8,128)(2,1)S(1)}, bf16[64,4096]{1,0:T(8,128)(2,1)S(1)}, u32[]{:S(2)}, u32[]{:S(2)}) collective-permute-start(bf16[64,4096]{1,0:T(8,128)(2,1)S(1)} %bitcast.8), channel_id=1, source_target_pairs={{0,5},{1,0},{4,1},{5,4},{8,13},{9,8},{12,9},{13,12},{2,7},{3,2},{6... | collective-permute-start | bytes 1572872 | tf_op jit(solution)/shard_map/ppermute | solution.py:153
  13.4 8.5 %collective-permute-start.4 = (bf16[64,4096]{1,0:T(8,128)(2,1)S(1)}, bf16[64,4096]{1,0:T(8,128)(2,1)S(1)}, u32[]{:S(2)}, u32[]{:S(2)}) collective-permute-start(bf16[64,4096]{1,0:T(8,128)(2,1)S(1)} %collective-permute-done.3.refs_5_), channel_id=1, source_target_pairs={{0,1},{1,0},{2,3},{3,2},{4,5},{5,4},{6,7},{7,6},{8,9},{9,8},{10,11... | collective-permute-start | bytes 1572872 | tf_op jit(solution)/shard_map/ppermute | solution.py:184
  13.8 4.7 %collective-permute-start.2 = (bf16[128,192]{1,0:T(8,128)(2,1)S(1)}, bf16[128,192]{1,0:T(8,128)(2,1)S(1)}, u32[]{:S(2)}, u32[]{:S(2)}) collective-permute-start(bf16[128,192]{1,0:T(8,128)(2,1)S(1)} %select_convert_fusion.refs_0_), channel_id=1, source_target_pairs={{0,4},{4,0},{8,12},{12,8},{1,5},{5,1},{9,13},{13,9},{2,6},{6,2},{1... | collective-permute-start | bytes 147464 | tf_op jit(solution)/shard_map/ppermute | solution.py:175
  15.9 6.1 %collective-permute-start.1 = (bf16[128,192]{1,0:T(8,128)(2,1)S(1)}, bf16[128,192]{1,0:T(8,128)(2,1)S(1)}, u32[]{:S(2)}, u32[]{:S(2)}) collective-permute-start(bf16[128,192]{1,0:T(8,128)(2,1)S(1)} %select_convert_fusion.refs_0_), channel_id=1, source_target_pairs={{0,12},{1,9},{4,8},{5,13},{8,4},{9,1},{12,0},{13,5},{2,14},{3,11},... | collective-permute-start | bytes 147464 | tf_op jit(solution)/shard_map/ppermute | solution.py:171
  23.1 1.9 %collective-permute-start.6 = (f32[2,128]{1,0:T(2,128)S(1)}, f32[2,128]{1,0:T(2,128)S(1)}, u32[]{:S(2)}, u32[]{:S(2)}) collective-permute-start(f32[2,128]{1,0:T(2,128)S(1)} %get-tuple-element.7), channel_id=1, source_target_pairs={{0,1},{1,0},{2,9},{3,8},{4,5},{5,4},{6,13},{7,12},{8,3},{9,2},{10,... | collective-permute-start | bytes 3080 | tf_op jit(solution)/shard_map/ppermute | solution.py:221
  23.1 3.6 %collective-permute-start.5 = (f32[2,128]{1,0:T(2,128)S(1)}, f32[2,128]{1,0:T(2,128)S(1)}, u32[]{:S(2)}, u32[]{:S(2)}) collective-permute-start(f32[2,128]{1,0:T(2,128)S(1)} %get-tuple-element.8), channel_id=1, source_target_pairs={{0,8},{1,9},{2,0},{3,1},{4,12},{5,13},{6,4},{7,5},{8,10},{9,11},{1... | collective-permute-start | bytes 3080 | tf_op jit(solution)/shard_map/ppermute | solution.py:221
  26.7 1.6 %collective-permute-start.7 = (f32[2,128]{1,0:T(2,128)S(1)}, f32[2,128]{1,0:T(2,128)S(1)}, u32[]{:S(2)}, u32[]{:S(2)}) collective-permute-start(f32[2,128]{1,0:T(2,128)S(1)} %add.92), channel_id=1, source_target_pairs={{0,1},{1,0},{2,3},{3,2},{4,5},{5,4},{6,7},{7,6},{8,9},{9,8},{10,11... | collective-permute-start | bytes 3080 | tf_op jit(solution)/shard_map/ppermute | solution.py:225

commit v3 on v1

v3 whole, which is shorter than its diff:
```python
import functools

import jax
import jax.numpy as jnp
from jax import lax
from jax.experimental import pallas as pl
from jax.experimental.pallas import tpu as pltpu
from jax.sharding import PartitionSpec as P


VMEM = pl.BlockSpec(memory_space=pltpu.VMEM)
LANES = 128
CHUNKS = 2


def dot_last(left, right):
    return lax.dot_general(
        left, right, (((1,), (1,)), ((), ())), preferred_element_type=jnp.float32
    )


def chunk_count(depth):
    return next(n for n in (CHUNKS, 1) if depth % (n * LANES) == 0)


def project_kernel(acts, grads, p_in, p_out, out, acts_v, grads_v, in_v, out_v, sems):
    rank = p_out.shape[1]
    count = chunk_count(acts.shape[2])
    size = acts.shape[2] // count

    def copies(n):
        part = (slice(None), pl.ds(pl.multiple_of(n * size, LANES), size))
        return [
            pltpu.make_async_copy(src.at[(0,) + part], dst.at[part], sems.at[2 * n + m])
            for m, (src, dst) in enumerate([(acts, acts_v), (p_in, in_v)])
        ]

    head = [
        pltpu.make_async_copy(src.at[0], dst, sems.at[2 * count + m])
        for m, (src, dst) in enumerate([(grads, grads_v), (p_out, out_v)])
    ]
    for copy in head:
        copy.start()
    for n in range(count):
        for copy in copies(n):
            copy.start()
    for copy in head:
        copy.wait()
    out[:rank] = dot_last(out_v[...], grads_v[...])
    out[rank:] = jnp.zeros_like(out[rank:])

    def step(n, carry):
        for copy in copies(n):
            copy.wait()
        part = pl.ds(pl.multiple_of(n * size, LANES), size)
        out[rank:] += dot_last(in_v[:, part], acts_v[:, part])
        return carry

    lax.fori_loop(0, count, step, 0)


def project(acts, grads, p_in, p_out):
    ranks = p_out.shape[1] + p_in.shape[1]
    toks = acts.shape[1]
    depth = acts.shape[2] + grads.shape[2]
    big = [pltpu.with_memory_space_constraint(x, pltpu.HBM) for x in (acts, grads, p_in, p_out)]
    return pl.pallas_call(
        project_kernel,
        out_shape=jax.ShapeDtypeStruct((ranks, toks), jnp.float32),
        in_specs=[pl.BlockSpec(memory_space=pltpu.HBM)] * 4,
        out_specs=VMEM,
        scratch_shapes=[pltpu.VMEM(x.shape[1:], x.dtype) for x in big]
        + [pltpu.SemaphoreType.DMA((2 * chunk_count(acts.shape[2]) + 2,))],
        compiler_params=pltpu.CompilerParams(vmem_limit_bytes=16 << 20),
        cost_estimate=pl.CostEstimate(
            flops=toks * ranks * depth,
            bytes_accessed=2 * depth * (toks + ranks // 2),
            transcendentals=0,
        ),
    )(*big)


def score_kernel(blocks, rank_out, bounds, *refs):
    sides, queries, out = refs[:blocks], refs[blocks:-1], refs[-1]
    toks = sides[0].shape[1]
    rows = bounds.shape[0]
    rank_in = sides[0].shape[0] - rank_out
    copies = LANES // rank_in
    lane = lax.broadcasted_iota(jnp.int32, (rows, toks), 1)
    total = None
    for c in range(blocks):
        inside = (lane >= bounds[:, 2 * c : 2 * c + 1]) & (lane < bounds[:, 2 * c + 1 : 2 * c + 2])
        g = sides[c][:rank_out].astype(jnp.float32)
        a = sides[c][rank_out:]
        spread = [jnp.where(inside, g[i : i + 1], 0.0) for i in range(rank_out)]
        weighted = jnp.concatenate(spread, axis=0).astype(jnp.bfloat16)
        part = dot_last(weighted, jnp.concatenate([a] * copies, axis=0))
        total = part if total is None else total + part
    column = lax.broadcasted_iota(jnp.int32, (rows, LANES), 1) // rank_in
    flat = []
    for i in range(0, rank_out, copies):
        tile = total[i * rows : (i + 1) * rows]
        for n in range(1, copies):
            tile = jnp.where(column == n, total[(i + n) * rows : (i + n + 1) * rows], tile)
        flat.append(tile)
    sketch = jnp.concatenate(flat, axis=1).astype(jnp.bfloat16)
    place = bounds[:, 2 * blocks : 2 * blocks + 1]
    got = [dot_last(sketch, q[0] if len(q.shape) == 3 else q[...]) for q in queries]
    ordered = []
    for n in range(len(got)):
        pick = got[0]
        for k in range(1, len(got)):
            pick = jnp.where((place ^ k) == n, got[k], pick)
        ordered.append(pick)
    out[...] = jnp.concatenate(ordered, axis=1)


def scores_of(sides, bounds, queries, rank_out):
    rows = bounds.shape[0]
    width = sum(q.shape[-2] for q in queries)
    depth = queries[0].shape[-1]
    return pl.pallas_call(
        functools.partial(score_kernel, len(sides), rank_out),
        out_shape=jax.ShapeDtypeStruct((rows, width), jnp.float32),
        in_specs=[VMEM] * (len(sides) + 1 + len(queries)),
        out_specs=VMEM,
        compiler_params=pltpu.CompilerParams(vmem_limit_bytes=24 << 20),
        cost_estimate=pl.CostEstimate(
            flops=2 * rows * depth * (width + len(sides) * sides[0].shape[1]),
            bytes_accessed=2 * depth * width,
            transcendentals=0,
        ),
    )(bounds, *sides, *queries)


def to_last(dps, cores, k):
    return [
        (i * cores + c, (i if c else i ^ k) * cores + (c - 1) % cores)
        for i in range(dps)
        for c in range(cores)
    ]


def hop_order(dps):
    return [dps // 2] + [k for k in range(dps - 1, 0, -1) if k != dps // 2]


def local(sizes, activations, out_grads, proj_in, proj_out, queries, lengths, owner_slot, pad_mask):
    dps, layers, cores = sizes
    pair = dps // layers
    assert cores > 1 and dps & (dps - 1) == 0
    toks = activations.shape[1]
    rank_out = proj_out.shape[1]
    own_rows = lengths.shape[0] // dps
    d, l, t = lax.axis_index("dp"), lax.axis_index("layer"), lax.axis_index("tensor")

    v = d % pair

    wanted = [queries]
    for k in range(1, pair):
        wanted.append(lax.ppermute(queries[0], ("dp", "tensor"), to_last(dps, cores, k)))

    partial_sides = project(
        activations, out_grads, proj_in, proj_out
    )
    both = partial_sides
    for k in range(1, cores):
        both = both + lax.ppermute(partial_sides, "tensor", [(i, i ^ k) for i in range(cores)])
    is_out = lax.broadcasted_iota(jnp.int32, both.shape, 0) < rank_out
    sides = jnp.where(is_out & (pad_mask == 0)[None], 0.0, both).astype(jnp.bfloat16)

    held, source = [sides], [d]
    for k in hop_order(dps):
        held.append(lax.ppermute(sides, ("dp", "tensor"), to_last(dps, cores, k)))
        source.append(d ^ k)

    rows = layers * own_rows
    padded = -(-rows // 8) * 8
    index = jnp.arange(padded, dtype=jnp.int32)
    slot = ((l ^ (index // own_rows)) * pair + v) * own_rows + index % own_rows
    slot = jnp.where(index < rows, slot, -1)
    ones = jnp.arange(lengths.shape[0])
    first = jnp.sum(jnp.where(ones[None, :] < ones[:, None], lengths[None, :], 0), axis=1)
    match = slot[:, None] == owner_slot[None, :]
    low = jnp.sum(jnp.where(match, first[None, :], 0), axis=1)
    size = jnp.sum(jnp.where(match, lengths[None, :], 0), axis=1)
    columns = []
    for src in source:
        columns += [low - src * toks, low + size - src * toks]
    columns.append(jnp.full_like(low, 1) * v)
    bounds = jnp.stack(columns, axis=1)

    served = scores_of(held, bounds, wanted, rank_out)

    whole = None
    for k in range(layers - 1, -1, -1):
        perm = []
        for su in range(layers):
            for sv in range(pair):
                for sl in range(layers):
                    src = ((su * pair + sv) * layers + sl) * cores
                    dst = (((sl ^ k) * pair + sv) * layers + su) * cores
                    perm.append((src + cores - 1, dst))
                    perm += [(src + c, src + c + 1) for c in range(cores - 1)]
        piece = served[k * own_rows : (k + 1) * own_rows]
        piece = lax.ppermute(piece, ("dp", "layer", "tensor"), perm)
        whole = piece if whole is None else whole + piece
    result = whole
    for k in range(1, cores):
        other = lax.ppermute(whole, "tensor", [(i, i ^ k) for i in range(cores)])
        result = jnp.where(t == k, other, result)
    return result


def solution(mesh):
    placed = (
        P("layer", ("groups", "dp"), "tensor"),
        P("layer", ("groups", "dp"), "tensor"),
        P("layer", None, "tensor"),
        P("layer", None, "tensor"),
        P("layer", "dp", None),
        P("groups"),
        P("groups"),
        P(("groups", "dp")),
    )
    sizes = tuple(mesh.shape[name] for name in ("dp", "layer", "tensor"))
    return jax.shard_map(
        functools.partial(local, sizes),
        mesh=mesh,
        in_specs=placed,
        out_specs=P(("groups", "dp"), "layer"),
        check_vma=False,
    )
```

time: 32.8 us -> 23.3 us (0.71)
  local copies, waits for them, and re-layouts: 6.19 us -> 0.75 us
  waiting for transfers between devices: 12.8 us -> 8.39 us
  Pallas kernels: 2.43 us -> 4.24 us
  starting transfers between devices: 10.2 us -> 8.71 us
    unnamed x16 -> x8, local copies, waits for them, and re-layouts: 5.75 us -> 0.01 us
    ppermute x5, waiting for transfers between devices: 11 us -> 5.4 us  [the longest x3 4.24 us: local(): held.append(lax.ppermute(sides, ('dp', 'tensor'), to_last(dps, cores, k)))]
    pallas_call x1, Pallas kernels: 1.24 us -> 2.97 us  [project(): pl.pallas_call(project_kernel, out_shape=jax.ShapeDtypeStruct((ranks, tok...]
    ppermute x5, starting transfers between devices: 7.74 us -> 6.04 us  [the longest x3 3.36 us: local(): held.append(lax.ppermute(sides, ('dp', 'tensor'), to_last(dps, cores, k)))]
    ppermute x2, waiting for transfers between devices: 1.77 us -> 2.98 us  [local(): piece = lax.ppermute(piece, ('dp', 'layer', 'tensor'), perm)]
    select_n x0 -> x1, other arithmetic: none -> 0.56 us  [local(): result = jnp.where(t == k, other, result)]
    add x1 -> x0, other arithmetic: 0.56 us -> none  [local(): result + lax.ppermute(whole, 'tensor', [(i, i ^ k) for i in range(cores)])]
    sub x3 -> x8, local copies, waits for them, and re-layouts: 0.24 us -> 0.65 us  [local(): columns += [low - src * toks, low + size - src * toks]]
  transfers between devices with their start and end apart: 8 -> 8, of which waited for: 5 -> 6; matrix products, arithmetic and copies ran while one was open for 2% -> 5% of each run, Pallas kernels for 0% -> 0%
where the time goes in v3:
time: 23.3 us; the launch traced here: 23.1 us
  starting transfers between devices  8.71 us (37%)
  waiting for transfers between devices  8.39 us (36%)
  Pallas kernels  4.24 us (18%)
  other arithmetic  0.99 us (4%)
  local copies, waits for them, and re-layouts  0.75 us (3%)
    ppermute x3, waiting for transfers between devices, local(): held.append(lax.ppermute(sides, ('dp', 'tensor'), to_last(dps, cores, k)))  4.24 us
    ppermute x3, starting transfers between devices, local(): held.append(lax.ppermute(sides, ('dp', 'tensor'), to_last(dps, cores, k)))  3.36 us
    ppermute x2, waiting for transfers between devices, local(): piece = lax.ppermute(piece, ('dp', 'layer', 'tensor'), perm)  2.98 us
    pallas_call x1, Pallas kernels, project(): pl.pallas_call(project_kernel, out_shape=jax.ShapeDtypeStruct((ranks, tok...  2.97 us
    ppermute x1, starting transfers between devices, local(): lax.ppermute(queries[0], ('dp', 'tensor'), to_last(dps, cores, k))  2.67 us
    ppermute x2, starting transfers between devices, local(): piece = lax.ppermute(piece, ('dp', 'layer', 'tensor'), perm)  2.1 us
    pallas_call x1, Pallas kernels, scores_of(): pl.pallas_call(functools.partial(score_kernel, len(sides), rank_out), out...  1.28 us
    ppermute x1, waiting for transfers between devices, local(): other = lax.ppermute(whole, 'tensor', [(i, i ^ k) for i in range(cores)])  1.16 us
  transfers between devices with their start and end apart: 8, of which 6 were waited for; matrix products, arithmetic and copies ran while one was open for 5% of the time, Pallas kernels for 0%

profile of v3, /device:TPU:0, one launch (start us, length us, event | category | flops | bytes accessed | tf_op | source)
XLA Modules:
  0.0 23.1 jit_solution(12654190181761661649)
XLA Ops:
  0.0 0.0 copy-start
  0.0 0.0 copy-start.3
  0.0 0.0 copy-start.1
  0.0 0.0 copy-start.2
  0.0 3.0 %shard_map.82 = f32[128,192]{1,0:T(8,128)S(1)} custom-call(bf16[1,192,7168]{2,1,0:T(8,128)(2,1)} %acts.1, bf16[1,192,2048]{2,1,0:T(8,128)(2,1)} %grads.1, bf16[1,64,7168]{2,1,0:T(8,128)(2,1)} %p_in.1, bf16[1,64,2048]{2,1,0:T(8,128)(2,1)} %p_out.1), custom_call_target="tpu_custom_call" | custom-call | flops 226492416 | bytes 4718592 | tf_op jit(solution)/shard_map/pallas_call | solution.py:67
  3.0 0.6 %collective-permute-start = (f32[128,192]{1,0:T(8,128)S(1)}, f32[128,192]{1,0:T(8,128)S(1)}, u32[]{:S(2)}, u32[]{:S(2)}) collective-permute-start(f32[128,192]{1,0:T(8,128)S(1)} %shard_map.82), channel_id=1, source_target_pairs={{0,1},{1,0},{2,3},{3,2},{4,5},{5,4},{6,7},{7,6},{8,9},{9,8},{10,11... | collective-permute-start | bytes 294920 | tf_op jit(solution)/shard_map/ppermute | solution.py:168
  3.6 0.0 copy-done
  3.6 2.7 %collective-permute-start.4 = (bf16[64,4096]{1,0:T(8,128)(2,1)S(1)}, bf16[64,4096]{1,0:T(8,128)(2,1)S(1)}, u32[]{:S(2)}, u32[]{:S(2)}) collective-permute-start(bf16[64,4096]{1,0:T(8,128)(2,1)S(1)} %bitcast.17), channel_id=1, source_target_pairs={{0,5},{1,0},{4,1},{5,4},{8,13},{9,8},{12,9},{13,12},{2,7},{3,2},{6... | collective-permute-start | bytes 1572872 | tf_op jit(solution)/shard_map/ppermute | solution.py:161
  6.2 0.0 copy-done.3
  6.2 0.0 copy-done.1
  6.2 0.1 select_reduce_fusion
  6.4 0.0 copy-done.2
  6.4 0.2 fusion.1
  6.6 0.0 collective-permute-done
  6.6 0.1 select_convert_fusion.refs_0_
  6.7 0.7 %collective-permute-start.3 = (bf16[128,192]{1,0:T(8,128)(2,1)S(1)}, bf16[128,192]{1,0:T(8,128)(2,1)S(1)}, u32[]{:S(2)}, u32[]{:S(2)}) collective-permute-start(bf16[128,192]{1,0:T(8,128)(2,1)S(1)} %select_convert_fusion.refs_0_), channel_id=1, source_target_pairs={{0,5},{1,0},{4,1},{5,4},{8,13},{9,8},{12,9},{13,12},{2,7},{3,2},{6... | collective-permute-start | bytes 147464 | tf_op jit(solution)/shard_map/ppermute | solution.py:174
  7.4 2.4 %collective-permute-start.2 = (bf16[128,192]{1,0:T(8,128)(2,1)S(1)}, bf16[128,192]{1,0:T(8,128)(2,1)S(1)}, u32[]{:S(2)}, u32[]{:S(2)}) collective-permute-start(bf16[128,192]{1,0:T(8,128)(2,1)S(1)} %select_convert_fusion.refs_0_), channel_id=1, source_target_pairs={{0,13},{1,0},{4,9},{5,4},{8,5},{9,8},{12,1},{13,12},{2,15},{3,2},{... | collective-permute-start | bytes 147464 | tf_op jit(solution)/shard_map/ppermute | solution.py:174
  9.7 0.3 %collective-permute-start.1 = (bf16[128,192]{1,0:T(8,128)(2,1)S(1)}, bf16[128,192]{1,0:T(8,128)(2,1)S(1)}, u32[]{:S(2)}, u32[]{:S(2)}) collective-permute-start(bf16[128,192]{1,0:T(8,128)(2,1)S(1)} %select_convert_fusion.refs_0_), channel_id=1, source_target_pairs={{0,9},{1,0},{4,13},{5,4},{8,1},{9,8},{12,5},{13,12},{2,11},{3,2},{... | collective-permute-start | bytes 147464 | tf_op jit(solution)/shard_map/ppermute | solution.py:174
  10.1 0.1 copy.22
  10.1 0.1 copy.23
  10.2 0.1 copy.20
  10.3 0.1 copy.18
  10.4 0.1 copy.21
  10.5 0.1 copy.19
  10.6 0.1 copy.24
  10.6 0.1 copy.17
  10.7 0.1 stack.2.bounds
  10.8 2.8 %collective-permute-done.3.refs_3_ = bf16[128,192]{1,0:T(8,128)(2,1)S(1)} collective-permute-done((bf16[128,192]{1,0:T(8,128)(2,1)S(1)}, bf16[128,192]{1,0:T(8,128)(2,1)S(1)}, u32[]{:S(2)}, u32[]{:S(2)}) %collective-permute-start.3) | collective-permute-done | bytes 49184 | tf_op jit(solution)/shard_map/ppermute | solution.py:174
  13.6 0.7 %collective-permute-done.2.refs_2_ = bf16[128,192]{1,0:T(8,128)(2,1)S(1)} collective-permute-done((bf16[128,192]{1,0:T(8,128)(2,1)S(1)}, bf16[128,192]{1,0:T(8,128)(2,1)S(1)}, u32[]{:S(2)}, u32[]{:S(2)}) %collective-permute-start.2) | collective-permute-done | bytes 49184 | tf_op jit(solution)/shard_map/ppermute | solution.py:174
  14.3 0.7 %collective-permute-done.1.refs_1_ = bf16[128,192]{1,0:T(8,128)(2,1)S(1)} collective-permute-done((bf16[128,192]{1,0:T(8,128)(2,1)S(1)}, bf16[128,192]{1,0:T(8,128)(2,1)S(1)}, u32[]{:S(2)}, u32[]{:S(2)}) %collective-permute-start.1) | collective-permute-done | bytes 49184 | tf_op jit(solution)/shard_map/ppermute | solution.py:174
  15.0 0.0 collective-permute-done.4.refs_5_
  15.0 1.3 %shard_map.83 = f32[8,128]{1,0:T(8,128)S(1)} custom-call(s32[8,9]{1,0:T(8,128)S(1)} %stack.2.bounds, bf16[128,192]{1,0:T(8,128)(2,1)S(1)} %select_convert_fusion.refs_0_, bf16[128,192]{1,0:T(8,128)(2,1)S(1)} %collective-permute-done.1.refs_1_, bf16[128,192]{1,0:T(8,128)(2,1)S(1)} %collective-permute-done.2.refs_2_, ...), custom_call_target="tpu_custom_call" | custom-call | flops 58720256 | bytes 1048576 | tf_op jit(solution)/shard_map/pallas_call | solution.py:122
  16.3 2.1 %collective-permute-start.6 = (f32[2,128]{1,0:T(2,128)S(1)}, f32[2,128]{1,0:T(2,128)S(1)}, u32[]{:S(2)}, u32[]{:S(2)}) collective-permute-start(f32[2,128]{1,0:T(2,128)S(1)} %get-tuple-element.9), channel_id=1, source_target_pairs={{1,0},{0,1},{3,8},{2,3},{5,4},{4,5},{7,12},{6,7},{9,2},{8,9},{11,1... | collective-permute-start | bytes 3080 | tf_op jit(solution)/shard_map/ppermute | solution.py:206
  18.4 0.0 collective-permute-start.5
  18.4 0.8 %collective-permute-done.6 = f32[2,128]{1,0:T(2,128)S(1)} collective-permute-done((f32[2,128]{1,0:T(2,128)S(1)}, f32[2,128]{1,0:T(2,128)S(1)}, u32[]{:S(2)}, u32[]{:S(2)}) %collective-permute-start.6) | collective-permute-done | bytes 1056 | tf_op jit(solution)/shard_map/ppermute | solution.py:206
  19.2 2.2 %collective-permute-done.5 = f32[2,128]{1,0:T(2,128)S(1)} collective-permute-done((f32[2,128]{1,0:T(2,128)S(1)}, f32[2,128]{1,0:T(2,128)S(1)}, u32[]{:S(2)}, u32[]{:S(2)}) %collective-permute-start.5) | collective-permute-done | bytes 1056 | tf_op jit(solution)/shard_map/ppermute | solution.py:206
  21.4 0.0 collective-permute-start.7
  21.4 1.2 %collective-permute-done.7 = f32[2,128]{1,0:T(2,128)S(1)} collective-permute-done((f32[2,128]{1,0:T(2,128)S(1)}, f32[2,128]{1,0:T(2,128)S(1)}, u32[]{:S(2)}, u32[]{:S(2)}) %collective-permute-start.7) | collective-permute-done | bytes 1056 | tf_op jit(solution)/shard_map/ppermute | solution.py:210
  22.6 0.6 %broadcast_select_fusion = f32[2,128]{1,0:T(2,128)} fusion(f32[2,128]{1,0:T(2,128)S(1)} %collective-permute-done.7, f32[2,128]{1,0:T(2,128)S(1)} %add.78, pred[]{:T(512)S(6)} %eq.26), kind=kLoop, calls=%fused_computation.13 | loop fusion | flops 256 | bytes 3073 | tf_op jit(solution)/shard_map/jit(_where)/select_n | solution.py:211
  (8 shorter events, 0.0 us)
Async XLA Ops:
  0.0 3.6 %copy-start = (bf16[1,64,4096]{2,1,0:T(8,128)(2,1)S(1)}, bf16[1,64,4096]{2,1,0:T(8,128)(2,1)}, u32[]{:S(2)}) copy-start(bf16[1,64,4096]{2,1,0:T(8,128)(2,1)} %refs_4_.1) | copy-start | bytes 1572868
  0.0 6.2 %copy-start.3 = (s32[192]{0:T(256)S(1)}, s32[192]{0:T(256)}, u32[]{:S(2)}) copy-start(s32[192]{0:T(256)} %param.15) | copy-start | bytes 2308
  0.0 6.2 %copy-start.1 = (s32[8]{0:T(128)S(1)}, s32[8]{0:T(128)}, u32[]{:S(2)}) copy-start(s32[8]{0:T(128)} %param.13) | copy-start | bytes 100
  0.0 6.4 %copy-start.2 = (s32[8]{0:T(128)S(1)}, s32[8]{0:T(128)}, u32[]{:S(2)}) copy-start(s32[8]{0:T(128)} %param.14) | copy-start | bytes 100
  3.0 3.6 %collective-permute-start = (f32[128,192]{1,0:T(8,128)S(1)}, f32[128,192]{1,0:T(8,128)S(1)}, u32[]{:S(2)}, u32[]{:S(2)}) collective-permute-start(f32[128,192]{1,0:T(8,128)S(1)} %shard_map.82), channel_id=1, source_target_pairs={{0,1},{1,0},{2,3},{3,2},{4,5},{5,4},{6,7},{7,6},{8,9},{9,8},{10,11... | collective-permute-start | bytes 294920 | tf_op jit(solution)/shard_map/ppermute | solution.py:168
  3.6 11.5 %collective-permute-start.4 = (bf16[64,4096]{1,0:T(8,128)(2,1)S(1)}, bf16[64,4096]{1,0:T(8,128)(2,1)S(1)}, u32[]{:S(2)}, u32[]{:S(2)}) collective-permute-start(bf16[64,4096]{1,0:T(8,128)(2,1)S(1)} %bitcast.17), channel_id=1, source_target_pairs={{0,5},{1,0},{4,1},{5,4},{8,13},{9,8},{12,9},{13,12},{2,7},{3,2},{6... | collective-permute-start | bytes 1572872 | tf_op jit(solution)/shard_map/ppermute | solution.py:161
  6.7 6.9 %collective-permute-start.3 = (bf16[128,192]{1,0:T(8,128)(2,1)S(1)}, bf16[128,192]{1,0:T(8,128)(2,1)S(1)}, u32[]{:S(2)}, u32[]{:S(2)}) collective-permute-start(bf16[128,192]{1,0:T(8,128)(2,1)S(1)} %select_convert_fusion.refs_0_), channel_id=1, source_target_pairs={{0,5},{1,0},{4,1},{5,4},{8,13},{9,8},{12,9},{13,12},{2,7},{3,2},{6... | collective-permute-start | bytes 147464 | tf_op jit(solution)/shard_map/ppermute | solution.py:174
  7.4 7.0 %collective-permute-start.2 = (bf16[128,192]{1,0:T(8,128)(2,1)S(1)}, bf16[128,192]{1,0:T(8,128)(2,1)S(1)}, u32[]{:S(2)}, u32[]{:S(2)}) collective-permute-start(bf16[128,192]{1,0:T(8,128)(2,1)S(1)} %select_convert_fusion.refs_0_), channel_id=1, source_target_pairs={{0,13},{1,0},{4,9},{5,4},{8,5},{9,8},{12,1},{13,12},{2,15},{3,2},{... | collective-permute-start | bytes 147464 | tf_op jit(solution)/shard_map/ppermute | solution.py:174
  9.7 5.3 %collective-permute-start.1 = (bf16[128,192]{1,0:T(8,128)(2,1)S(1)}, bf16[128,192]{1,0:T(8,128)(2,1)S(1)}, u32[]{:S(2)}, u32[]{:S(2)}) collective-permute-start(bf16[128,192]{1,0:T(8,128)(2,1)S(1)} %select_convert_fusion.refs_0_), channel_id=1, source_target_pairs={{0,9},{1,0},{4,13},{5,4},{8,1},{9,8},{12,5},{13,12},{2,11},{3,2},{... | collective-permute-start | bytes 147464 | tf_op jit(solution)/shard_map/ppermute | solution.py:174
  16.3 2.9 %collective-permute-start.6 = (f32[2,128]{1,0:T(2,128)S(1)}, f32[2,128]{1,0:T(2,128)S(1)}, u32[]{:S(2)}, u32[]{:S(2)}) collective-permute-start(f32[2,128]{1,0:T(2,128)S(1)} %get-tuple-element.9), channel_id=1, source_target_pairs={{1,0},{0,1},{3,8},{2,3},{5,4},{4,5},{7,12},{6,7},{9,2},{8,9},{11,1... | collective-permute-start | bytes 3080 | tf_op jit(solution)/shard_map/ppermute | solution.py:206
  18.4 3.0 %collective-permute-start.5 = (f32[2,128]{1,0:T(2,128)S(1)}, f32[2,128]{1,0:T(2,128)S(1)}, u32[]{:S(2)}, u32[]{:S(2)}) collective-permute-start(f32[2,128]{1,0:T(2,128)S(1)} %get-tuple-element.10), channel_id=1, source_target_pairs={{1,8},{0,1},{3,0},{2,3},{5,12},{4,5},{7,4},{6,7},{9,10},{8,9},{11,... | collective-permute-start | bytes 3080 | tf_op jit(solution)/shard_map/ppermute | solution.py:206
  21.4 1.2 %collective-permute-start.7 = (f32[2,128]{1,0:T(2,128)S(1)}, f32[2,128]{1,0:T(2,128)S(1)}, u32[]{:S(2)}, u32[]{:S(2)}) collective-permute-start(f32[2,128]{1,0:T(2,128)S(1)} %add.78), channel_id=1, source_target_pairs={{0,1},{1,0},{2,3},{3,2},{4,5},{5,4},{6,7},{7,6},{8,9},{9,8},{10,11... | collective-permute-start | bytes 3080 | tf_op jit(solution)/shard_map/ppermute | solution.py:210

commit v4 on v3

--- a/solution.py
+++ b/solution.py
@@ -80,22 +80,29 @@
     )(*big)
 
 
-def score_kernel(blocks, rank_out, bounds, *refs):
-    sides, queries, out = refs[:blocks], refs[blocks:-1], refs[-1]
+def gather_kernel(first, count, scored, rank_out, *refs):
+    refs = list(refs)
+    bounds = refs.pop(0)
+    before = None if first == 0 else refs.pop(0)
+    sides, queries, out = refs[:count], refs[count:-1], refs[-1]
     toks = sides[0].shape[1]
     rows = bounds.shape[0]
     rank_in = sides[0].shape[0] - rank_out
     copies = LANES // rank_in
     lane = lax.broadcasted_iota(jnp.int32, (rows, toks), 1)
-    total = None
-    for c in range(blocks):
-        inside = (lane >= bounds[:, 2 * c : 2 * c + 1]) & (lane < bounds[:, 2 * c + 1 : 2 * c + 2])
+    total = None if before is None else before[...]
+    for c in range(count):
+        low, high = 2 * (first + c), 2 * (first + c) + 1
+        inside = (lane >= bounds[:, low : low + 1]) & (lane < bounds[:, high : high + 1])
         g = sides[c][:rank_out].astype(jnp.float32)
         a = sides[c][rank_out:]
         spread = [jnp.where(inside, g[i : i + 1], 0.0) for i in range(rank_out)]
         weighted = jnp.concatenate(spread, axis=0).astype(jnp.bfloat16)
         part = dot_last(weighted, jnp.concatenate([a] * copies, axis=0))
         total = part if total is None else total + part
+    if not scored:
+        out[...] = total
+        return
     column = lax.broadcasted_iota(jnp.int32, (rows, LANES), 1) // rank_in
     flat = []
     for i in range(0, rank_out, copies):
@@ -104,7 +111,7 @@
             tile = jnp.where(column == n, total[(i + n) * rows : (i + n + 1) * rows], tile)
         flat.append(tile)
     sketch = jnp.concatenate(flat, axis=1).astype(jnp.bfloat16)
-    place = bounds[:, 2 * blocks : 2 * blocks + 1]
+    place = bounds[:, bounds.shape[1] - 1 :]
     got = [dot_last(sketch, q[0] if len(q.shape) == 3 else q[...]) for q in queries]
     ordered = []
     for n in range(len(got)):
@@ -115,22 +122,32 @@
     out[...] = jnp.concatenate(ordered, axis=1)
 
 
-def scores_of(sides, bounds, queries, rank_out):
+def gather(bounds, before, first, sides, queries, rank_out):
     rows = bounds.shape[0]
+    args = [bounds] + ([] if before is None else [before]) + list(sides) + list(queries)
     width = sum(q.shape[-2] for q in queries)
-    depth = queries[0].shape[-1]
+    depth = queries[0].shape[-1] if queries else 0
+    shape = (rows, width) if queries else (rows * rank_out, LANES)
     return pl.pallas_call(
-        functools.partial(score_kernel, len(sides), rank_out),
-        out_shape=jax.ShapeDtypeStruct((rows, width), jnp.float32),
-        in_specs=[VMEM] * (len(sides) + 1 + len(queries)),
+        functools.partial(gather_kernel, first, len(sides), bool(queries), rank_out),
+        out_shape=jax.ShapeDtypeStruct(shape, jnp.float32),
+        in_specs=[VMEM] * len(args),
         out_specs=VMEM,
         compiler_params=pltpu.CompilerParams(vmem_limit_bytes=24 << 20),
         cost_estimate=pl.CostEstimate(
-            flops=2 * rows * depth * (width + len(sides) * sides[0].shape[1]),
-            bytes_accessed=2 * depth * width,
+            flops=2 * rows * (depth * width + rank_out * LANES * len(sides) * sides[0].shape[1]),
+            bytes_accessed=2 * depth * width + rows * rank_out * LANES * 4,
             transcendentals=0,
         ),
-    )(bounds, *sides, *queries)
+    )(*args)
+
+
+def scores_of(sides, bounds, queries, rank_out):
+    total = None
+    for first, last in [(n, n + 1) for n in range(len(sides))]:
+        asked = queries if last == len(sides) else []
+        total = gather(bounds, total, first, sides[first:last], asked, rank_out)
+    return total
 
 
 def to_last(dps, cores, k):
@@ -142,7 +159,7 @@
 
 
 def hop_order(dps):
-    return [dps // 2] + [k for k in range(dps - 1, 0, -1) if k != dps // 2]
+    return list(range(dps - 1, 0, -1))
 
 
 def local(sizes, activations, out_grads, proj_in, proj_out, queries, lengths, owner_slot, pad_mask):
@@ -193,7 +210,7 @@
     served = scores_of(held, bounds, wanted, rank_out)
 
     whole = None
-    for k in range(layers - 1, -1, -1):
+    for k in range(layers):
         perm = []
         for su in range(layers):
             for sv in range(pair):

time: 23.3 us -> 24.6 us (1.056)
  the two profiles are of different devices: /device:TPU:0 before, /device:TPU:3 now
where the time goes in v4:
time: 24.6 us; the launch traced here: 24.4 us
  waiting for transfers between devices  9.34 us (38%)
  starting transfers between devices  8.82 us (36%)
  Pallas kernels  4.4 us (18%)
  other arithmetic  0.98 us (4%)
  local copies, waits for them, and re-layouts  0.75 us (3%)
    ppermute x3, waiting for transfers between devices, local(): held.append(lax.ppermute(sides, ('dp', 'tensor'), to_last(dps, cores, k)))  6.82 us
    ppermute x1, starting transfers between devices, local(): other = lax.ppermute(whole, 'tensor', [(i, i ^ k) for i in range(cores)])  4.13 us
    ppermute x3, starting transfers between devices, local(): held.append(lax.ppermute(sides, ('dp', 'tensor'), to_last(dps, cores, k)))  3.84 us
    pallas_call x1, Pallas kernels, project(): pl.pallas_call(project_kernel, out_shape=jax.ShapeDtypeStruct((ranks, tok...  2.97 us
    pallas_call x4, Pallas kernels, gather(): pl.pallas_call(functools.partial(gather_kernel, first, len(sides), bool(q...  1.43 us
    ppermute x2, waiting for transfers between devices, local(): piece = lax.ppermute(piece, ('dp', 'layer', 'tensor'), perm)  1.15 us
    ppermute x1, waiting for transfers between devices, local(): other = lax.ppermute(whole, 'tensor', [(i, i ^ k) for i in range(cores)])  0.82 us
    ppermute x1, starting transfers between devices, local(): lax.ppermute(partial_sides, 'tensor', [(i, i ^ k) for i in range(cores)])  0.74 us
  transfers between devices with their start and end apart: 8, of which 4 were waited for; matrix products, arithmetic and copies ran while one was open for 5% of the time, Pallas kernels for 3%

profile of v4, /device:TPU:3, one launch (start us, length us, event | category | flops | bytes accessed | tf_op | source)
XLA Modules:
  0.0 24.4 jit_solution(14714937679051972678)
XLA Ops:
  0.0 0.0 copy-start
  0.0 0.0 copy-start.3
  0.0 0.0 copy-start.1
  0.0 0.0 copy-start.2
  0.0 3.0 %shard_map.82 = f32[128,192]{1,0:T(8,128)S(1)} custom-call(bf16[1,192,7168]{2,1,0:T(8,128)(2,1)} %acts.1, bf16[1,192,2048]{2,1,0:T(8,128)(2,1)} %grads.1, bf16[1,64,7168]{2,1,0:T(8,128)(2,1)} %p_in.1, bf16[1,64,2048]{2,1,0:T(8,128)(2,1)} %p_out.1), custom_call_target="tpu_custom_call" | custom-call | flops 226492416 | bytes 4718592 | tf_op jit(solution)/shard_map/pallas_call | solution.py:67
  3.0 0.7 %collective-permute-start = (f32[128,192]{1,0:T(8,128)S(1)}, f32[128,192]{1,0:T(8,128)S(1)}, u32[]{:S(2)}, u32[]{:S(2)}) collective-permute-start(f32[128,192]{1,0:T(8,128)S(1)} %shard_map.82), channel_id=1, source_target_pairs={{0,1},{1,0},{2,3},{3,2},{4,5},{5,4},{6,7},{7,6},{8,9},{9,8},{10,11... | collective-permute-start | bytes 294920 | tf_op jit(solution)/shard_map/ppermute | solution.py:185
  3.7 0.0 copy-done
  3.7 0.1 collective-permute-start.4
  3.8 0.0 copy-done.3
  3.8 0.0 copy-done.1
  3.8 0.1 select_reduce_fusion
  4.0 0.0 copy-done.2
  4.0 0.2 fusion.1
  4.2 0.6 %collective-permute-done = f32[128,192]{1,0:T(8,128)S(1)} collective-permute-done((f32[128,192]{1,0:T(8,128)S(1)}, f32[128,192]{1,0:T(8,128)S(1)}, u32[]{:S(2)}, u32[]{:S(2)}) %collective-permute-start) | collective-permute-done | bytes 98336 | tf_op jit(solution)/shard_map/ppermute | solution.py:185
  4.7 0.1 select_convert_fusion.refs_1_
  4.8 1.1 %collective-permute-start.3 = (bf16[128,192]{1,0:T(8,128)(2,1)S(1)}, bf16[128,192]{1,0:T(8,128)(2,1)S(1)}, u32[]{:S(2)}, u32[]{:S(2)}) collective-permute-start(bf16[128,192]{1,0:T(8,128)(2,1)S(1)} %select_convert_fusion.refs_1_), channel_id=1, source_target_pairs={{0,5},{1,0},{4,1},{5,4},{8,13},{9,8},{12,9},{13,12},{2,7},{3,2},{6... | collective-permute-start | bytes 147464 | tf_op jit(solution)/shard_map/ppermute | solution.py:191
  5.9 0.6 %collective-permute-start.2 = (bf16[128,192]{1,0:T(8,128)(2,1)S(1)}, bf16[128,192]{1,0:T(8,128)(2,1)S(1)}, u32[]{:S(2)}, u32[]{:S(2)}) collective-permute-start(bf16[128,192]{1,0:T(8,128)(2,1)S(1)} %select_convert_fusion.refs_1_), channel_id=1, source_target_pairs={{0,9},{1,0},{4,13},{5,4},{8,1},{9,8},{12,5},{13,12},{2,11},{3,2},{... | collective-permute-start | bytes 147464 | tf_op jit(solution)/shard_map/ppermute | solution.py:191
  6.6 2.1 %collective-permute-start.1 = (bf16[128,192]{1,0:T(8,128)(2,1)S(1)}, bf16[128,192]{1,0:T(8,128)(2,1)S(1)}, u32[]{:S(2)}, u32[]{:S(2)}) collective-permute-start(bf16[128,192]{1,0:T(8,128)(2,1)S(1)} %select_convert_fusion.refs_1_), channel_id=1, source_target_pairs={{0,13},{1,0},{4,9},{5,4},{8,5},{9,8},{12,1},{13,12},{2,15},{3,2},{... | collective-permute-start | bytes 147464 | tf_op jit(solution)/shard_map/ppermute | solution.py:191
  8.7 0.1 copy.22
  8.7 0.1 copy.23
  8.8 0.1 copy.20
  8.9 0.1 copy.18
  9.0 0.1 copy.21
  9.1 0.1 copy.19
  9.2 0.1 copy.24
  9.2 0.1 copy.17
  9.3 0.1 stack.2.refs_0_
  9.4 0.3 %shard_map.83.refs_1_ = f32[512,128]{1,0:T(8,128)S(1)} custom-call(s32[8,9]{1,0:T(8,128)S(1)} %stack.2.refs_0_, bf16[128,192]{1,0:T(8,128)(2,1)S(1)} %select_convert_fusion.refs_1_), custom_call_target="tpu_custom_call" | custom-call | flops 25165824 | bytes 262144 | tf_op jit(solution)/shard_map/pallas_call | solution.py:131
  9.7 6.8 %collective-permute-done.1.refs_2_ = bf16[128,192]{1,0:T(8,128)(2,1)S(1)} collective-permute-done((bf16[128,192]{1,0:T(8,128)(2,1)S(1)}, bf16[128,192]{1,0:T(8,128)(2,1)S(1)}, u32[]{:S(2)}, u32[]{:S(2)}) %collective-permute-start.1) | collective-permute-done | bytes 49184 | tf_op jit(solution)/shard_map/ppermute | solution.py:191
  16.5 0.3 %shard_map.84.refs_1_ = f32[512,128]{1,0:T(8,128)S(1)} custom-call(s32[8,9]{1,0:T(8,128)S(1)} %stack.2.refs_0_, f32[512,128]{1,0:T(8,128)S(1)} %shard_map.83.refs_1_, bf16[128,192]{1,0:T(8,128)(2,1)S(1)} %collective-permute-done.1.refs_2_), custom_call_target="tpu_custom_call" | custom-call | flops 25165824 | bytes 262144 | tf_op jit(solution)/shard_map/pallas_call | solution.py:131
  16.7 0.0 collective-permute-done.2.refs_2_
  16.8 0.3 %shard_map.85.refs_1_ = f32[512,128]{1,0:T(8,128)S(1)} custom-call(s32[8,9]{1,0:T(8,128)S(1)} %stack.2.refs_0_, f32[512,128]{1,0:T(8,128)S(1)} %shard_map.84.refs_1_, bf16[128,192]{1,0:T(8,128)(2,1)S(1)} %collective-permute-done.2.refs_2_), custom_call_target="tpu_custom_call" | custom-call | flops 25165824 | bytes 262144 | tf_op jit(solution)/shard_map/pallas_call | solution.py:131
  17.0 0.0 collective-permute-done.3.refs_2_
  17.0 0.0 collective-permute-done.4.refs_4_
  17.0 0.6 %shard_map.86 = f32[8,128]{1,0:T(8,128)S(1)} custom-call(s32[8,9]{1,0:T(8,128)S(1)} %stack.2.refs_0_, f32[512,128]{1,0:T(8,128)S(1)} %shard_map.85.refs_1_, bf16[128,192]{1,0:T(8,128)(2,1)S(1)} %collective-permute-done.3.refs_2_, bf16[1,64,4096]{2,1,0:T(8,128)(2,1)S(1)} %copy-done, bf16[64,4096]{1,0:T(8,128)(2,1)S(1)} %collective-permute-done.4.refs_4_), custom_call_target="tpu_custom_call" | custom-call | flops 33554432 | bytes 1310720 | tf_op jit(solution)/shard_map/pallas_call | solution.py:131
  17.7 0.0 collective-permute-start.6
  17.7 0.0 collective-permute-start.5
  17.7 1.1 %collective-permute-done.6 = f32[2,128]{1,0:T(2,128)S(1)} collective-permute-done((f32[2,128]{1,0:T(2,128)S(1)}, f32[2,128]{1,0:T(2,128)S(1)}, u32[]{:S(2)}, u32[]{:S(2)}) %collective-permute-start.6) | collective-permute-done | bytes 1056 | tf_op jit(solution)/shard_map/ppermute | solution.py:223
  18.9 0.0 collective-permute-done.5
  18.9 4.1 %collective-permute-start.7 = (f32[2,128]{1,0:T(2,128)S(1)}, f32[2,128]{1,0:T(2,128)S(1)}, u32[]{:S(2)}, u32[]{:S(2)}) collective-permute-start(f32[2,128]{1,0:T(2,128)S(1)} %add.78), channel_id=1, source_target_pairs={{0,1},{1,0},{2,3},{3,2},{4,5},{5,4},{6,7},{7,6},{8,9},{9,8},{10,11... | collective-permute-start | bytes 3080 | tf_op jit(solution)/shard_map/ppermute | solution.py:227
  23.0 0.8 %collective-permute-done.7 = f32[2,128]{1,0:T(2,128)S(1)} collective-permute-done((f32[2,128]{1,0:T(2,128)S(1)}, f32[2,128]{1,0:T(2,128)S(1)}, u32[]{:S(2)}, u32[]{:S(2)}) %collective-permute-start.7) | collective-permute-done | bytes 1056 | tf_op jit(solution)/shard_map/ppermute | solution.py:227
  23.8 0.6 %broadcast_select_fusion = f32[2,128]{1,0:T(2,128)} fusion(f32[2,128]{1,0:T(2,128)S(1)} %collective-permute-done.7, f32[2,128]{1,0:T(2,128)S(1)} %add.78, pred[]{:T(512)S(6)} %eq.26), kind=kLoop, calls=%fused_computation.13 | loop fusion | flops 256 | bytes 3073 | tf_op jit(solution)/shard_map/jit(_where)/select_n | solution.py:228
  (8 shorter events, 0.0 us)
Async XLA Ops:
  0.0 3.7 %copy-start = (bf16[1,64,4096]{2,1,0:T(8,128)(2,1)S(1)}, bf16[1,64,4096]{2,1,0:T(8,128)(2,1)}, u32[]{:S(2)}) copy-start(bf16[1,64,4096]{2,1,0:T(8,128)(2,1)} %refs_3_.1) | copy-start | bytes 1572868
  0.0 3.8 %copy-start.3 = (s32[192]{0:T(256)S(1)}, s32[192]{0:T(256)}, u32[]{:S(2)}) copy-start(s32[192]{0:T(256)} %param.15) | copy-start | bytes 2308
  0.0 3.8 %copy-start.1 = (s32[8]{0:T(128)S(1)}, s32[8]{0:T(128)}, u32[]{:S(2)}) copy-start(s32[8]{0:T(128)} %param.13) | copy-start | bytes 100
  0.0 3.9 %copy-start.2 = (s32[8]{0:T(128)S(1)}, s32[8]{0:T(128)}, u32[]{:S(2)}) copy-start(s32[8]{0:T(128)} %param.14) | copy-start | bytes 100
  3.0 1.7 %collective-permute-start = (f32[128,192]{1,0:T(8,128)S(1)}, f32[128,192]{1,0:T(8,128)S(1)}, u32[]{:S(2)}, u32[]{:S(2)}) collective-permute-start(f32[128,192]{1,0:T(8,128)S(1)} %shard_map.82), channel_id=1, source_target_pairs={{0,1},{1,0},{2,3},{3,2},{4,5},{5,4},{6,7},{7,6},{8,9},{9,8},{10,11... | collective-permute-start | bytes 294920 | tf_op jit(solution)/shard_map/ppermute | solution.py:185
  3.7 13.3 %collective-permute-start.4 = (bf16[64,4096]{1,0:T(8,128)(2,1)S(1)}, bf16[64,4096]{1,0:T(8,128)(2,1)S(1)}, u32[]{:S(2)}, u32[]{:S(2)}) collective-permute-start(bf16[64,4096]{1,0:T(8,128)(2,1)S(1)} %bitcast.17), channel_id=1, source_target_pairs={{0,5},{1,0},{4,1},{5,4},{8,13},{9,8},{12,9},{13,12},{2,7},{3,2},{6... | collective-permute-start | bytes 1572872 | tf_op jit(solution)/shard_map/ppermute | solution.py:178
  4.8 12.2 %collective-permute-start.3 = (bf16[128,192]{1,0:T(8,128)(2,1)S(1)}, bf16[128,192]{1,0:T(8,128)(2,1)S(1)}, u32[]{:S(2)}, u32[]{:S(2)}) collective-permute-start(bf16[128,192]{1,0:T(8,128)(2,1)S(1)} %select_convert_fusion.refs_1_), channel_id=1, source_target_pairs={{0,5},{1,0},{4,1},{5,4},{8,13},{9,8},{12,9},{13,12},{2,7},{3,2},{6... | collective-permute-start | bytes 147464 | tf_op jit(solution)/shard_map/ppermute | solution.py:191
  5.9 10.8 %collective-permute-start.2 = (bf16[128,192]{1,0:T(8,128)(2,1)S(1)}, bf16[128,192]{1,0:T(8,128)(2,1)S(1)}, u32[]{:S(2)}, u32[]{:S(2)}) collective-permute-start(bf16[128,192]{1,0:T(8,128)(2,1)S(1)} %select_convert_fusion.refs_1_), channel_id=1, source_target_pairs={{0,9},{1,0},{4,13},{5,4},{8,1},{9,8},{12,5},{13,12},{2,11},{3,2},{... | collective-permute-start | bytes 147464 | tf_op jit(solution)/shard_map/ppermute | solution.py:191
  6.6 9.9 %collective-permute-start.1 = (bf16[128,192]{1,0:T(8,128)(2,1)S(1)}, bf16[128,192]{1,0:T(8,128)(2,1)S(1)}, u32[]{:S(2)}, u32[]{:S(2)}) collective-permute-start(bf16[128,192]{1,0:T(8,128)(2,1)S(1)} %select_convert_fusion.refs_1_), channel_id=1, source_target_pairs={{0,13},{1,0},{4,9},{5,4},{8,5},{9,8},{12,1},{13,12},{2,15},{3,2},{... | collective-permute-start | bytes 147464 | tf_op jit(solution)/shard_map/ppermute | solution.py:191
  17.7 1.2 %collective-permute-start.6 = (f32[2,128]{1,0:T(2,128)S(1)}, f32[2,128]{1,0:T(2,128)S(1)}, u32[]{:S(2)}, u32[]{:S(2)}) collective-permute-start(f32[2,128]{1,0:T(2,128)S(1)} %get-tuple-element.9), channel_id=1, source_target_pairs={{1,8},{0,1},{3,0},{2,3},{5,12},{4,5},{7,4},{6,7},{9,10},{8,9},{11,... | collective-permute-start | bytes 3080 | tf_op jit(solution)/shard_map/ppermute | solution.py:223
  17.7 1.2 %collective-permute-start.5 = (f32[2,128]{1,0:T(2,128)S(1)}, f32[2,128]{1,0:T(2,128)S(1)}, u32[]{:S(2)}, u32[]{:S(2)}) collective-permute-start(f32[2,128]{1,0:T(2,128)S(1)} %get-tuple-element.10), channel_id=1, source_target_pairs={{1,0},{0,1},{3,8},{2,3},{5,4},{4,5},{7,12},{6,7},{9,2},{8,9},{11,1... | collective-permute-start | bytes 3080 | tf_op jit(solution)/shard_map/ppermute | solution.py:223
  18.9 5.0 %collective-permute-start.7 = (f32[2,128]{1,0:T(2,128)S(1)}, f32[2,128]{1,0:T(2,128)S(1)}, u32[]{:S(2)}, u32[]{:S(2)}) collective-permute-start(f32[2,128]{1,0:T(2,128)S(1)} %add.78), channel_id=1, source_target_pairs={{0,1},{1,0},{2,3},{3,2},{4,5},{5,4},{6,7},{7,6},{8,9},{9,8},{10,11... | collective-permute-start | bytes 3080 | tf_op jit(solution)/shard_map/ppermute | solution.py:227

commit v5 on v3

--- a/solution.py
+++ b/solution.py
@@ -80,22 +80,21 @@
     )(*big)
 
 
-def score_kernel(blocks, rank_out, bounds, *refs):
-    sides, queries, out = refs[:blocks], refs[blocks:-1], refs[-1]
-    toks = sides[0].shape[1]
-    rows = bounds.shape[0]
-    rank_in = sides[0].shape[0] - rank_out
+def sketch_kernel(cores, rank_out, bounds, mask, *refs):
+    shares, outs = refs[:cores], refs[cores:]
+    rows, toks = bounds.shape[0], mask.shape[1]
+    rank_in = shares[0].shape[0] - rank_out
     copies = LANES // rank_in
     lane = lax.broadcasted_iota(jnp.int32, (rows, toks), 1)
-    total = None
-    for c in range(blocks):
-        inside = (lane >= bounds[:, 2 * c : 2 * c + 1]) & (lane < bounds[:, 2 * c + 1 : 2 * c + 2])
-        g = sides[c][:rank_out].astype(jnp.float32)
-        a = sides[c][rank_out:]
-        spread = [jnp.where(inside, g[i : i + 1], 0.0) for i in range(rank_out)]
-        weighted = jnp.concatenate(spread, axis=0).astype(jnp.bfloat16)
-        part = dot_last(weighted, jnp.concatenate([a] * copies, axis=0))
-        total = part if total is None else total + part
+    inside = (lane >= bounds[:, 0:1]) & (lane < bounds[:, 1:2]) & (mask[...] != 0)
+    both = shares[0][...]
+    for share in shares[1:]:
+        both = both + share[...]
+    both = both.astype(jnp.bfloat16)
+    g, a = both[:rank_out].astype(jnp.float32), both[rank_out:]
+    spread = [jnp.where(inside, g[i : i + 1], 0.0) for i in range(rank_out)]
+    weighted = jnp.concatenate(spread, axis=0).astype(jnp.bfloat16)
+    total = dot_last(weighted, jnp.concatenate([a] * copies, axis=0))
     column = lax.broadcasted_iota(jnp.int32, (rows, LANES), 1) // rank_in
     flat = []
     for i in range(0, rank_out, copies):
@@ -103,9 +102,38 @@
         for n in range(1, copies):
             tile = jnp.where(column == n, total[(i + n) * rows : (i + n + 1) * rows], tile)
         flat.append(tile)
-    sketch = jnp.concatenate(flat, axis=1).astype(jnp.bfloat16)
-    place = bounds[:, 2 * blocks : 2 * blocks + 1]
-    got = [dot_last(sketch, q[0] if len(q.shape) == 3 else q[...]) for q in queries]
+    sketch = jnp.concatenate(flat, axis=1)
+    part = rows // len(outs)
+    for n, out in enumerate(outs):
+        out[...] = sketch[n * part : (n + 1) * part].astype(out.dtype)
+
+
+def sketches_of(shares, bounds, mask, rank_out, pair):
+    rows = bounds.shape[0]
+    depth = rank_out * (shares[0].shape[0] - rank_out)
+    return pl.pallas_call(
+        functools.partial(sketch_kernel, len(shares), rank_out),
+        out_shape=[jax.ShapeDtypeStruct((rows // pair, depth), jnp.bfloat16)] * pair,
+        in_specs=[VMEM] * (len(shares) + 2),
+        out_specs=[VMEM] * pair,
+        compiler_params=pltpu.CompilerParams(vmem_limit_bytes=24 << 20),
+        cost_estimate=pl.CostEstimate(
+            flops=2 * rows * depth * mask.shape[1],
+            bytes_accessed=2 * rows * depth,
+            transcendentals=0,
+        ),
+    )(bounds, mask, *shares)
+
+
+def score_kernel(count, bounds, *refs):
+    sketches, queries, out = refs[:count], refs[count:-1], refs[-1]
+    total = sketches[0][...].astype(jnp.float32)
+    for sketch in sketches[1:]:
+        total = total + sketch[...].astype(jnp.float32)
+    total = total.astype(jnp.bfloat16)
+    rows = total.shape[0]
+    place = bounds[:rows, 2:3]
+    got = [dot_last(total, q[0] if len(q.shape) == 3 else q[...]) for q in queries]
     ordered = []
     for n in range(len(got)):
         pick = got[0]
@@ -115,22 +143,19 @@
     out[...] = jnp.concatenate(ordered, axis=1)
 
 
-def scores_of(sides, bounds, queries, rank_out):
-    rows = bounds.shape[0]
+def scores_of(sketches, bounds, queries):
+    rows, depth = sketches[0].shape
     width = sum(q.shape[-2] for q in queries)
-    depth = queries[0].shape[-1]
     return pl.pallas_call(
-        functools.partial(score_kernel, len(sides), rank_out),
+        functools.partial(score_kernel, len(sketches)),
         out_shape=jax.ShapeDtypeStruct((rows, width), jnp.float32),
-        in_specs=[VMEM] * (len(sides) + 1 + len(queries)),
+        in_specs=[VMEM] * (1 + len(sketches) + len(queries)),
         out_specs=VMEM,
         compiler_params=pltpu.CompilerParams(vmem_limit_bytes=24 << 20),
         cost_estimate=pl.CostEstimate(
-            flops=2 * rows * depth * (width + len(sides) * sides[0].shape[1]),
-            bytes_accessed=2 * depth * width,
-            transcendentals=0,
+            flops=2 * rows * depth * width, bytes_accessed=2 * depth * width, transcendentals=0
         ),
-    )(bounds, *sides, *queries)
+    )(bounds, *sketches, *queries)
 
 
 def to_last(dps, cores, k):
@@ -141,8 +166,29 @@
     ]
 
 
+def home_perm(sizes, k):
+    dps, layers, cores = sizes
+    pair = dps // layers
+    perm = []
+    for u in range(layers):
+        for v in range(pair):
+            for l in range(layers):
+                src = ((u * pair + v) * layers + l) * cores
+                dst = (((l ^ k) * pair + v) * layers + u) * cores
+                side = ((u * pair + v) * layers + (l ^ 1)) * cores
+                chain = [(src + c, src + c + 1) for c in range(cores - 1)]
+                if k or layers != 2:
+                    perm += [(src + cores - 1, dst)] + chain
+                elif u != l:
+                    perm += [(src + cores - 1, dst), (src, side)]
+                    perm += [(src + c, src + c + 1) for c in range(1, cores - 1)]
+                else:
+                    perm += [(src + cores - 1, side + 1)] + chain
+    return perm
+
+
 def hop_order(dps):
-    return [dps // 2] + [k for k in range(dps - 1, 0, -1) if k != dps // 2]
+    return [1] + list(range(dps - 1, 1, -1))
 
 
 def local(sizes, activations, out_grads, proj_in, proj_out, queries, lengths, owner_slot, pad_mask):
@@ -163,52 +209,49 @@
     partial_sides = project(
         activations, out_grads, proj_in, proj_out
     )
-    both = partial_sides
+    shares = [partial_sides]
     for k in range(1, cores):
-        both = both + lax.ppermute(partial_sides, "tensor", [(i, i ^ k) for i in range(cores)])
-    is_out = lax.broadcasted_iota(jnp.int32, both.shape, 0) < rank_out
-    sides = jnp.where(is_out & (pad_mask == 0)[None], 0.0, both).astype(jnp.bfloat16)
-
-    held, source = [sides], [d]
+        shares.append(lax.ppermute(partial_sides, "tensor", [(i, i ^ k) for i in range(cores)]))
+
+    rows = layers * own_rows
+    index = jnp.arange(pair * rows, dtype=jnp.int32)
+    turn = index // rows
+    half = l ^ (index % rows // own_rows)
+    slot = (half * pair + (v ^ turn)) * own_rows + index % own_rows
+    count = jnp.arange(lengths.shape[0])
+    first = jnp.sum(jnp.where(count[None, :] < count[:, None], lengths[None, :], 0), axis=1)
+    match = slot[:, None] == owner_slot[None, :]
+    low = jnp.sum(jnp.where(match, first[None, :], 0), axis=1) - d * toks
+    high = low + jnp.sum(jnp.where(match, lengths[None, :], 0), axis=1)
+    column = jnp.arange(3)[None, :]
+    bounds = jnp.where(column == 0, low[:, None], jnp.where(column == 1, high[:, None], v))
+
+    sketches = sketches_of(shares, bounds, pad_mask[None], rank_out, pair)
+
+    held = [sketches[0]]
     for k in hop_order(dps):
-        held.append(lax.ppermute(sides, ("dp", "tensor"), to_last(dps, cores, k)))
-        source.append(d ^ k)
-
-    rows = layers * own_rows
-    padded = -(-rows // 8) * 8
-    index = jnp.arange(padded, dtype=jnp.int32)
-    slot = ((l ^ (index // own_rows)) * pair + v) * own_rows + index % own_rows
-    slot = jnp.where(index < rows, slot, -1)
-    ones = jnp.arange(lengths.shape[0])
-    first = jnp.sum(jnp.where(ones[None, :] < ones[:, None], lengths[None, :], 0), axis=1)
-    match = slot[:, None] == owner_slot[None, :]
-    low = jnp.sum(jnp.where(match, first[None, :], 0), axis=1)
-    size = jnp.sum(jnp.where(match, lengths[None, :], 0), axis=1)
-    columns = []
-    for src in source:
-        columns += [low - src * toks, low + size - src * toks]
-    columns.append(jnp.full_like(low, 1) * v)
-    bounds = jnp.stack(columns, axis=1)
-
-    served = scores_of(held, bounds, wanted, rank_out)
+        held.append(lax.ppermute(sketches[k % pair], ("dp", "tensor"), to_last(dps, cores, k)))
+
+    served = scores_of(held, bounds, wanted)
 
     whole = None
-    for k in range(layers - 1, -1, -1):
-        perm = []
-        for su in range(layers):
-            for sv in range(pair):
-                for sl in range(layers):
-                    src = ((su * pair + sv) * layers + sl) * cores
-                    dst = (((sl ^ k) * pair + sv) * layers + su) * cores
-                    perm.append((src + cores - 1, dst))
-                    perm += [(src + c, src + c + 1) for c in range(cores - 1)]
+    for k in range(layers):
+        perm = home_perm(sizes, k)
         piece = served[k * own_rows : (k + 1) * own_rows]
         piece = lax.ppermute(piece, ("dp", "layer", "tensor"), perm)
+        if k == 0 and layers == 2:
+            piece = jnp.where(d // pair == l, 0.0, piece)
         whole = piece if whole is None else whole + piece
-    result = whole
+    if layers == 2:
+        kept = jnp.where(d // pair == l, served[:own_rows], 0.0)
+    else:
+        kept = jnp.zeros_like(whole)
+    parts = jnp.where(t == 0, whole, jnp.where(t == cores - 1, kept, 0.0))
+    result = parts
     for k in range(1, cores):
-        other = lax.ppermute(whole, "tensor", [(i, i ^ k) for i in range(cores)])
-        result = jnp.where(t == k, other, result)
+        result = result + lax.ppermute(
+            parts, "tensor", [(i, i ^ k) for i in range(cores)]
+        )
     return result
 
 

time: 23.3 us -> 21.7 us (0.931)
  waiting for transfers between devices: 8.39 us -> 6.7 us
  starting transfers between devices: 8.71 us -> 10.2 us
  local copies, waits for them, and re-layouts: 0.75 us -> 0.02 us
  Pallas kernels: 4.24 us -> 3.67 us
    ppermute x2, starting transfers between devices: 2.1 us -> 3.63 us  [local(): piece = lax.ppermute(piece, ('dp', 'layer', 'tensor'), perm)]
    ppermute x2, waiting for transfers between devices: 2.98 us -> 1.79 us  [local(): piece = lax.ppermute(piece, ('dp', 'layer', 'tensor'), perm)]
    sub x8 -> x0, local copies, waits for them, and re-layouts: 0.65 us -> none  [local(): columns += [low - src * toks, low + size - src * toks]]
    add x1 -> x3, other arithmetic: 0.01 us -> 0.58 us  [the longest x1 0.56 us: local(): result + lax.ppermute(parts, 'tensor', [(i, i ^ k) for i in range(cores)])]
    pallas_call x1 -> x2, Pallas kernels: 1.28 us -> 0.71 us  [the longest x1 0.44 us: scores_of(): pl.pallas_call(functools.partial(score_kernel, len(sketches)), out_shape=...]
    ppermute x4, waiting for transfers between devices: 5.4 us -> 4.9 us  [the longest x3 3.74 us: local(): lax.ppermute(sketches[k % pair], ('dp', 'tensor'), to_last(dps, cores, k))]
    select_n x2, other arithmetic: 0.57 us -> 0.08 us  [the longest x1 0.07 us: local(): jnp.where(column == 0, low[:, None], jnp.where(column == 1, high[:, None]...]
  transfers between devices with their start and end apart: 8 -> 8, of which waited for: 6 -> 5; matrix products, arithmetic and copies ran while one was open for 5% -> 2% of each run, Pallas kernels for 0% -> 1%
where the time goes in v5:
time: 21.7 us; the launch traced here: 21.6 us
  starting transfers between devices  10.2 us (47%)
  waiting for transfers between devices  6.7 us (31%)
  Pallas kernels  3.67 us (17%)
  other arithmetic  0.97 us (4%)
    ppermute x3, waiting for transfers between devices, local(): lax.ppermute(sketches[k % pair], ('dp', 'tensor'), to_last(dps, cores, k))  3.74 us
    ppermute x2, starting transfers between devices, local(): piece = lax.ppermute(piece, ('dp', 'layer', 'tensor'), perm)  3.63 us
    ppermute x3, starting transfers between devices, local(): lax.ppermute(sketches[k % pair], ('dp', 'tensor'), to_last(dps, cores, k))  3.3 us
    pallas_call x1, Pallas kernels, project(): pl.pallas_call(project_kernel, out_shape=jax.ShapeDtypeStruct((ranks, tok...  2.97 us
    ppermute x1, starting transfers between devices, local(): lax.ppermute(queries[0], ('dp', 'tensor'), to_last(dps, cores, k))  2.67 us
    ppermute x2, waiting for transfers between devices, local(): piece = lax.ppermute(piece, ('dp', 'layer', 'tensor'), perm)  1.79 us
    ppermute x1, waiting for transfers between devices, local(): lax.ppermute(parts, 'tensor', [(i, i ^ k) for i in range(cores)])  1.16 us
    ppermute x1, starting transfers between devices, local(): lax.ppermute(partial_sides, 'tensor', [(i, i ^ k) for i in range(cores)])  0.58 us
  transfers between devices with their start and end apart: 8, of which 5 were waited for; matrix products, arithmetic and copies ran while one was open for 2% of the time, Pallas kernels for 1%

profile of v5, /device:TPU:0, one launch (start us, length us, event | category | flops | bytes accessed | tf_op | source)
XLA Modules:
  0.0 21.6 jit_solution(17497600403246029693)
XLA Ops:
  0.0 0.0 copy-start
  0.0 0.0 copy-start.2
  0.0 0.0 copy-start.3
  0.0 0.0 copy-start.1
  0.0 3.0 %shard_map.82.refs_0_ = f32[128,192]{1,0:T(8,128)S(1)} custom-call(bf16[1,192,7168]{2,1,0:T(8,128)(2,1)} %acts.1, bf16[1,192,2048]{2,1,0:T(8,128)(2,1)} %grads.1, bf16[1,64,7168]{2,1,0:T(8,128)(2,1)} %p_in.1, bf16[1,64,2048]{2,1,0:T(8,128)(2,1)} %p_out.1), custom_call_target="tpu_custom_call" | custom-call | flops 226492416 | bytes 4718592 | tf_op jit(solution)/shard_map/pallas_call | solution.py:67
  3.0 0.6 %collective-permute-start = (f32[128,192]{1,0:T(8,128)S(1)}, f32[128,192]{1,0:T(8,128)S(1)}, u32[]{:S(2)}, u32[]{:S(2)}) collective-permute-start(f32[128,192]{1,0:T(8,128)S(1)} %shard_map.82.refs_0_), channel_id=1, source_target_pairs={{0,1},{1,0},{2,3},{3,2},{4,5},{5,4},{6,7},{7,6},{8,9},{9,8},{10,11... | collective-permute-start | bytes 294920 | tf_op jit(solution)/shard_map/ppermute | solution.py:214
  3.6 0.0 copy-done
  3.6 2.7 %collective-permute-start.4 = (bf16[64,4096]{1,0:T(8,128)(2,1)S(1)}, bf16[64,4096]{1,0:T(8,128)(2,1)S(1)}, u32[]{:S(2)}, u32[]{:S(2)}) collective-permute-start(bf16[64,4096]{1,0:T(8,128)(2,1)S(1)} %bitcast.2), channel_id=1, source_target_pairs={{0,5},{1,0},{4,1},{5,4},{8,13},{9,8},{12,9},{13,12},{2,7},{3,2},{6... | collective-permute-start | bytes 1572872 | tf_op jit(solution)/shard_map/ppermute | solution.py:207
  6.2 0.0 copy-done.2
  6.2 0.1 select_reduce_fusion
  6.4 0.0 copy-done.3
  6.4 0.2 fusion.1
  6.6 0.1 select_select_fusion.bounds
  6.7 0.0 collective-permute-done.refs_1_
  6.7 0.0 copy-done.1
  6.7 0.3 %shard_map.83 = (bf16[4,4096]{1,0:T(4,128)(2,1)S(1)}, bf16[4,4096]{1,0:T(4,128)(2,1)S(1)}) custom-call(s32[8,3]{1,0:T(8,128)S(1)} %select_select_fusion.bounds, s32[1,192]{1,0:T(1,128)S(1)} %bitcast.3, f32[128,192]{1,0:T(8,128)S(1)} %shard_map.82.refs_0_, f32[128,192]{1,0:T(8,128)S(1)} %collective-permute-done.refs_1_), custom_call_target="tpu_custom_call" | custom-call | flops 12582912 | bytes 65536 | tf_op jit(solution)/shard_map/pallas_call | solution.py:114
  6.9 1.6 %collective-permute-start.3 = (bf16[4,4096]{1,0:T(4,128)(2,1)S(1)}, bf16[4,4096]{1,0:T(4,128)(2,1)S(1)}, u32[]{:S(2)}, u32[]{:S(2)}) collective-permute-start(bf16[4,4096]{1,0:T(4,128)(2,1)S(1)} %get-tuple-element.7.refs_0_), channel_id=1, source_target_pairs={{0,9},{1,0},{4,13},{5,4},{8,1},{9,8},{12,5},{13,12},{2,11},{3,2},{... | collective-permute-start | bytes 98312 | tf_op jit(solution)/shard_map/ppermute | solution.py:233
  8.6 1.4 %collective-permute-start.2 = (bf16[4,4096]{1,0:T(4,128)(2,1)S(1)}, bf16[4,4096]{1,0:T(4,128)(2,1)S(1)}, u32[]{:S(2)}, u32[]{:S(2)}) collective-permute-start(bf16[4,4096]{1,0:T(4,128)(2,1)S(1)} %get-tuple-element.8), channel_id=1, source_target_pairs={{0,13},{1,0},{4,9},{5,4},{8,5},{9,8},{12,1},{13,12},{2,15},{3,2},{... | collective-permute-start | bytes 98312 | tf_op jit(solution)/shard_map/ppermute | solution.py:233
  9.9 0.3 %collective-permute-start.1 = (bf16[4,4096]{1,0:T(4,128)(2,1)S(1)}, bf16[4,4096]{1,0:T(4,128)(2,1)S(1)}, u32[]{:S(2)}, u32[]{:S(2)}) collective-permute-start(bf16[4,4096]{1,0:T(4,128)(2,1)S(1)} %get-tuple-element.8), channel_id=1, source_target_pairs={{0,5},{1,0},{4,1},{5,4},{8,13},{9,8},{12,9},{13,12},{2,7},{3,2},{6... | collective-permute-start | bytes 98312 | tf_op jit(solution)/shard_map/ppermute | solution.py:233
  10.2 3.0 %collective-permute-done.3.refs_3_ = bf16[4,4096]{1,0:T(4,128)(2,1)S(1)} collective-permute-done((bf16[4,4096]{1,0:T(4,128)(2,1)S(1)}, bf16[4,4096]{1,0:T(4,128)(2,1)S(1)}, u32[]{:S(2)}, u32[]{:S(2)}) %collective-permute-start.3) | collective-permute-done | bytes 32800 | tf_op jit(solution)/shard_map/ppermute | solution.py:233
  13.3 0.4 %collective-permute-done.2.refs_2_ = bf16[4,4096]{1,0:T(4,128)(2,1)S(1)} collective-permute-done((bf16[4,4096]{1,0:T(4,128)(2,1)S(1)}, bf16[4,4096]{1,0:T(4,128)(2,1)S(1)}, u32[]{:S(2)}, u32[]{:S(2)}) %collective-permute-start.2) | collective-permute-done | bytes 32800 | tf_op jit(solution)/shard_map/ppermute | solution.py:233
  13.6 0.4 %collective-permute-done.1.refs_1_ = bf16[4,4096]{1,0:T(4,128)(2,1)S(1)} collective-permute-done((bf16[4,4096]{1,0:T(4,128)(2,1)S(1)}, bf16[4,4096]{1,0:T(4,128)(2,1)S(1)}, u32[]{:S(2)}, u32[]{:S(2)}) %collective-permute-start.1) | collective-permute-done | bytes 32800 | tf_op jit(solution)/shard_map/ppermute | solution.py:233
  14.0 0.0 collective-permute-done.4.refs_5_
  14.0 0.4 %shard_map.84 = f32[4,128]{1,0:T(4,128)S(1)} custom-call(s32[8,3]{1,0:T(8,128)S(1)} %select_select_fusion.bounds, bf16[4,4096]{1,0:T(4,128)(2,1)S(1)} %get-tuple-element.7.refs_0_, bf16[4,4096]{1,0:T(4,128)(2,1)S(1)} %collective-permute-done.1.refs_1_, bf16[4,4096]{1,0:T(4,128)(2,1)S(1)} %collective-permute-done.2.refs_2_, ...), custom_call_target="tpu_custom_call" | custom-call | flops 4194304 | bytes 1048576 | tf_op jit(solution)/shard_map/pallas_call | solution.py:149
  14.4 2.4 %collective-permute-start.5 = (f32[2,128]{1,0:T(2,128)S(1)}, f32[2,128]{1,0:T(2,128)S(1)}, u32[]{:S(2)}, u32[]{:S(2)}) collective-permute-start(f32[2,128]{1,0:T(2,128)S(1)} %get-tuple-element.13), channel_id=1, source_target_pairs={{1,3},{0,1},{3,8},{2,0},{5,7},{4,5},{7,12},{6,4},{9,2},{8,10},{11,... | collective-permute-start | bytes 3080 | tf_op jit(solution)/shard_map/ppermute | solution.py:241
  16.9 1.2 %collective-permute-start.6 = (f32[2,128]{1,0:T(2,128)S(1)}, f32[2,128]{1,0:T(2,128)S(1)}, u32[]{:S(2)}, u32[]{:S(2)}) collective-permute-start(f32[2,128]{1,0:T(2,128)S(1)} %get-tuple-element.14), channel_id=1, source_target_pairs={{1,8},{0,1},{3,0},{2,3},{5,12},{4,5},{7,4},{6,7},{9,10},{8,9},{11,... | collective-permute-start | bytes 3080 | tf_op jit(solution)/shard_map/ppermute | solution.py:241
  18.1 0.0 collective-permute-done.5
  18.1 1.8 %collective-permute-done.6 = f32[2,128]{1,0:T(2,128)S(1)} collective-permute-done((f32[2,128]{1,0:T(2,128)S(1)}, f32[2,128]{1,0:T(2,128)S(1)}, u32[]{:S(2)}, u32[]{:S(2)}) %collective-permute-start.6) | collective-permute-done | bytes 1056 | tf_op jit(solution)/shard_map/ppermute | solution.py:241
  19.9 0.0 collective-permute-start.7
  19.9 1.2 %collective-permute-done.7 = f32[2,128]{1,0:T(2,128)S(1)} collective-permute-done((f32[2,128]{1,0:T(2,128)S(1)}, f32[2,128]{1,0:T(2,128)S(1)}, u32[]{:S(2)}, u32[]{:S(2)}) %collective-permute-start.7) | collective-permute-done | bytes 1056 | tf_op jit(solution)/shard_map/ppermute | solution.py:252
  21.0 0.6 %add.67 = f32[2,128]{1,0:T(2,128)} add(f32[2,128]{1,0:T(2,128)S(1)} %select_select_fusion.1, f32[2,128]{1,0:T(2,128)S(1)} %collective-permute-done.7) | non-fusion elementwise | flops 256 | bytes 3072 | tf_op jit(solution)/shard_map/add | solution.py:252
  (5 shorter events, 0.0 us)
Async XLA Ops:
  0.0 3.6 %copy-start = (bf16[1,64,4096]{2,1,0:T(8,128)(2,1)S(1)}, bf16[1,64,4096]{2,1,0:T(8,128)(2,1)}, u32[]{:S(2)}) copy-start(bf16[1,64,4096]{2,1,0:T(8,128)(2,1)} %refs_4_.1) | copy-start | bytes 1572868
  0.0 6.2 %copy-start.2 = (s32[8]{0:T(128)S(1)}, s32[8]{0:T(128)}, u32[]{:S(2)}) copy-start(s32[8]{0:T(128)} %param.13) | copy-start | bytes 100
  0.0 6.4 %copy-start.3 = (s32[8]{0:T(128)S(1)}, s32[8]{0:T(128)}, u32[]{:S(2)}) copy-start(s32[8]{0:T(128)} %param.14) | copy-start | bytes 100
  0.0 6.7 %copy-start.1 = (s32[192]{0:T(256)S(1)}, s32[192]{0:T(256)}, u32[]{:S(2)}) copy-start(s32[192]{0:T(256)} %param.15) | copy-start | bytes 2308
  3.0 3.7 %collective-permute-start = (f32[128,192]{1,0:T(8,128)S(1)}, f32[128,192]{1,0:T(8,128)S(1)}, u32[]{:S(2)}, u32[]{:S(2)}) collective-permute-start(f32[128,192]{1,0:T(8,128)S(1)} %shard_map.82.refs_0_), channel_id=1, source_target_pairs={{0,1},{1,0},{2,3},{3,2},{4,5},{5,4},{6,7},{7,6},{8,9},{9,8},{10,11... | collective-permute-start | bytes 294920 | tf_op jit(solution)/shard_map/ppermute | solution.py:214
  3.6 10.4 %collective-permute-start.4 = (bf16[64,4096]{1,0:T(8,128)(2,1)S(1)}, bf16[64,4096]{1,0:T(8,128)(2,1)S(1)}, u32[]{:S(2)}, u32[]{:S(2)}) collective-permute-start(bf16[64,4096]{1,0:T(8,128)(2,1)S(1)} %bitcast.2), channel_id=1, source_target_pairs={{0,5},{1,0},{4,1},{5,4},{8,13},{9,8},{12,9},{13,12},{2,7},{3,2},{6... | collective-permute-start | bytes 1572872 | tf_op jit(solution)/shard_map/ppermute | solution.py:207
  6.9 6.3 %collective-permute-start.3 = (bf16[4,4096]{1,0:T(4,128)(2,1)S(1)}, bf16[4,4096]{1,0:T(4,128)(2,1)S(1)}, u32[]{:S(2)}, u32[]{:S(2)}) collective-permute-start(bf16[4,4096]{1,0:T(4,128)(2,1)S(1)} %get-tuple-element.7.refs_0_), channel_id=1, source_target_pairs={{0,9},{1,0},{4,13},{5,4},{8,1},{9,8},{12,5},{13,12},{2,11},{3,2},{... | collective-permute-start | bytes 98312 | tf_op jit(solution)/shard_map/ppermute | solution.py:233
  8.6 5.1 %collective-permute-start.2 = (bf16[4,4096]{1,0:T(4,128)(2,1)S(1)}, bf16[4,4096]{1,0:T(4,128)(2,1)S(1)}, u32[]{:S(2)}, u32[]{:S(2)}) collective-permute-start(bf16[4,4096]{1,0:T(4,128)(2,1)S(1)} %get-tuple-element.8), channel_id=1, source_target_pairs={{0,13},{1,0},{4,9},{5,4},{8,5},{9,8},{12,1},{13,12},{2,15},{3,2},{... | collective-permute-start | bytes 98312 | tf_op jit(solution)/shard_map/ppermute | solution.py:233
  9.9 4.1 %collective-permute-start.1 = (bf16[4,4096]{1,0:T(4,128)(2,1)S(1)}, bf16[4,4096]{1,0:T(4,128)(2,1)S(1)}, u32[]{:S(2)}, u32[]{:S(2)}) collective-permute-start(bf16[4,4096]{1,0:T(4,128)(2,1)S(1)} %get-tuple-element.8), channel_id=1, source_target_pairs={{0,5},{1,0},{4,1},{5,4},{8,13},{9,8},{12,9},{13,12},{2,7},{3,2},{6... | collective-permute-start | bytes 98312 | tf_op jit(solution)/shard_map/ppermute | solution.py:233
  14.4 3.6 %collective-permute-start.5 = (f32[2,128]{1,0:T(2,128)S(1)}, f32[2,128]{1,0:T(2,128)S(1)}, u32[]{:S(2)}, u32[]{:S(2)}) collective-permute-start(f32[2,128]{1,0:T(2,128)S(1)} %get-tuple-element.13), channel_id=1, source_target_pairs={{1,3},{0,1},{3,8},{2,0},{5,7},{4,5},{7,12},{6,4},{9,2},{8,10},{11,... | collective-permute-start | bytes 3080 | tf_op jit(solution)/shard_map/ppermute | solution.py:241
  16.9 3.0 %collective-permute-start.6 = (f32[2,128]{1,0:T(2,128)S(1)}, f32[2,128]{1,0:T(2,128)S(1)}, u32[]{:S(2)}, u32[]{:S(2)}) collective-permute-start(f32[2,128]{1,0:T(2,128)S(1)} %get-tuple-element.14), channel_id=1, source_target_pairs={{1,8},{0,1},{3,0},{2,3},{5,12},{4,5},{7,4},{6,7},{9,10},{8,9},{11,... | collective-permute-start | bytes 3080 | tf_op jit(solution)/shard_map/ppermute | solution.py:241
  19.9 1.2 %collective-permute-start.7 = (f32[2,128]{1,0:T(2,128)S(1)}, f32[2,128]{1,0:T(2,128)S(1)}, u32[]{:S(2)}, u32[]{:S(2)}) collective-permute-start(f32[2,128]{1,0:T(2,128)S(1)} %select_select_fusion.1), channel_id=1, source_target_pairs={{0,1},{1,0},{2,3},{3,2},{4,5},{5,4},{6,7},{7,6},{8,9},{9,8},{10,11... | collective-permute-start | bytes 3080 | tf_op jit(solution)/shard_map/ppermute | solution.py:252

commit v6 on v5

--- a/solution.py
+++ b/solution.py
@@ -23,7 +23,7 @@
     return next(n for n in (CHUNKS, 1) if depth % (n * LANES) == 0)
 
 
-def project_kernel(acts, grads, p_in, p_out, out, acts_v, grads_v, in_v, out_v, sems):
+def project_kernel(acts, grads, p_in, p_out, out, sent, acts_v, grads_v, in_v, out_v, sems):
     rank = p_out.shape[1]
     count = chunk_count(acts.shape[2])
     size = acts.shape[2] // count
@@ -57,6 +57,7 @@
         return carry
 
     lax.fori_loop(0, count, step, 0)
+    sent[...] = out[...].astype(sent.dtype)
 
 
 def project(acts, grads, p_in, p_out):
@@ -66,9 +67,9 @@
     big = [pltpu.with_memory_space_constraint(x, pltpu.HBM) for x in (acts, grads, p_in, p_out)]
     return pl.pallas_call(
         project_kernel,
-        out_shape=jax.ShapeDtypeStruct((ranks, toks), jnp.float32),
+        out_shape=[jax.ShapeDtypeStruct((ranks, toks), x) for x in (jnp.float32, jnp.bfloat16)],
         in_specs=[pl.BlockSpec(memory_space=pltpu.HBM)] * 4,
-        out_specs=VMEM,
+        out_specs=[VMEM] * 2,
         scratch_shapes=[pltpu.VMEM(x.shape[1:], x.dtype) for x in big]
         + [pltpu.SemaphoreType.DMA((2 * chunk_count(acts.shape[2]) + 2,))],
         compiler_params=pltpu.CompilerParams(vmem_limit_bytes=16 << 20),
@@ -89,7 +90,7 @@
     inside = (lane >= bounds[:, 0:1]) & (lane < bounds[:, 1:2]) & (mask[...] != 0)
     both = shares[0][...]
     for share in shares[1:]:
-        both = both + share[...]
+        both = both + share[...].astype(jnp.float32)
     both = both.astype(jnp.bfloat16)
     g, a = both[:rank_out].astype(jnp.float32), both[rank_out:]
     spread = [jnp.where(inside, g[i : i + 1], 0.0) for i in range(rank_out)]
@@ -125,29 +126,32 @@
     )(bounds, mask, *shares)
 
 
-def score_kernel(count, bounds, *refs):
+def score_kernel(count, worker, bounds, *refs):
     sketches, queries, out = refs[:count], refs[count:-1], refs[-1]
-    total = sketches[0][...].astype(jnp.float32)
-    for sketch in sketches[1:]:
-        total = total + sketch[...].astype(jnp.float32)
-    total = total.astype(jnp.bfloat16)
-    rows = total.shape[0]
-    place = bounds[:rows, 2:3]
-    got = [dot_last(total, q[0] if len(q.shape) == 3 else q[...]) for q in queries]
-    ordered = []
-    for n in range(len(got)):
-        pick = got[0]
-        for k in range(1, len(got)):
-            pick = jnp.where((place ^ k) == n, got[k], pick)
-        ordered.append(pick)
-    out[...] = jnp.concatenate(ordered, axis=1)
-
-
-def scores_of(sketches, bounds, queries):
+    out[...] = jnp.zeros_like(out)
+
+    @pl.when(lax.axis_index("tensor") == worker)
+    def _():
+        total = sketches[0][...].astype(jnp.float32)
+        for sketch in sketches[1:]:
+            total = total + sketch[...].astype(jnp.float32)
+        total = total.astype(jnp.bfloat16)
+        place = bounds[: total.shape[0], 2:3]
+        got = [dot_last(total, q[0] if len(q.shape) == 3 else q[...]) for q in queries]
+        ordered = []
+        for n in range(len(got)):
+            pick = got[0]
+            for k in range(1, len(got)):
+                pick = jnp.where((place ^ k) == n, got[k], pick)
+            ordered.append(pick)
+        out[...] = jnp.concatenate(ordered, axis=1)
+
+
+def scores_of(sketches, bounds, queries, worker):
     rows, depth = sketches[0].shape
     width = sum(q.shape[-2] for q in queries)
     return pl.pallas_call(
-        functools.partial(score_kernel, len(sketches)),
+        functools.partial(score_kernel, len(sketches), worker),
         out_shape=jax.ShapeDtypeStruct((rows, width), jnp.float32),
         in_specs=[VMEM] * (1 + len(sketches) + len(queries)),
         out_specs=VMEM,
@@ -206,18 +210,18 @@
     for k in range(1, pair):
         wanted.append(lax.ppermute(queries[0], ("dp", "tensor"), to_last(dps, cores, k)))
 
-    partial_sides = project(
+    partial_sides, sent_sides = project(
         activations, out_grads, proj_in, proj_out
     )
     shares = [partial_sides]
     for k in range(1, cores):
-        shares.append(lax.ppermute(partial_sides, "tensor", [(i, i ^ k) for i in range(cores)]))
+        shares.append(lax.ppermute(sent_sides, "tensor", [(i, i ^ k) for i in range(cores)]))
 
     rows = layers * own_rows
     index = jnp.arange(pair * rows, dtype=jnp.int32)
     turn = index // rows
     half = l ^ (index % rows // own_rows)
-    slot = (half * pair + (v ^ turn)) * own_rows + index % own_rows
+    slot = (half * pair + (v + turn) % pair) * own_rows + index % own_rows
     count = jnp.arange(lengths.shape[0])
     first = jnp.sum(jnp.where(count[None, :] < count[:, None], lengths[None, :], 0), axis=1)
     match = slot[:, None] == owner_slot[None, :]
@@ -230,9 +234,14 @@
 
     held = [sketches[0]]
     for k in hop_order(dps):
-        held.append(lax.ppermute(sketches[k % pair], ("dp", "tensor"), to_last(dps, cores, k)))
-
-    served = scores_of(held, bounds, wanted)
+        perm = [
+            (i * cores + c, (i if c else (i + k) % dps) * cores + (c - 1) % cores)
+            for i in range(dps)
+            for c in range(cores)
+        ]
+        held.append(lax.ppermute(sketches[k % pair], ("dp", "tensor"), perm))
+
+    served = scores_of(held, bounds, wanted, cores - 1)
 
     whole = None
     for k in range(layers):

time: 21.7 us -> 22.1 us (1.018)
  starting transfers between devices: 10.2 us -> 10.9 us
  Pallas kernels: 3.67 us -> 3.25 us
    ppermute x2, starting transfers between devices: 3.63 us -> 4.42 us  [local(): piece = lax.ppermute(piece, ('dp', 'layer', 'tensor'), perm)]
    pallas_call x2, Pallas kernels: 3.41 us -> 2.97 us  [the longest x1 2.97 us: project(): pl.pallas_call(project_kernel, out_shape=[jax.ShapeDtypeStruct((ranks, to...]
where the time goes in v6:
time: 22.1 us; the launch traced here: 22 us
  starting transfers between devices  10.9 us (49%)
  waiting for transfers between devices  6.77 us (31%)
  Pallas kernels  3.25 us (15%)
  other arithmetic  0.97 us (4%)
    ppermute x2, starting transfers between devices, local(): piece = lax.ppermute(piece, ('dp', 'layer', 'tensor'), perm)  4.42 us
    ppermute x3, waiting for transfers between devices, local(): held.append(lax.ppermute(sketches[k % pair], ('dp', 'tensor'), perm))  3.82 us
    ppermute x3, starting transfers between devices, local(): held.append(lax.ppermute(sketches[k % pair], ('dp', 'tensor'), perm))  3.22 us
    pallas_call x1, Pallas kernels, project(): pl.pallas_call(project_kernel, out_shape=[jax.ShapeDtypeStruct((ranks, to...  2.97 us
    ppermute x1, starting transfers between devices, local(): lax.ppermute(queries[0], ('dp', 'tensor'), to_last(dps, cores, k))  2.67 us
    ppermute x2, waiting for transfers between devices, local(): piece = lax.ppermute(piece, ('dp', 'layer', 'tensor'), perm)  1.79 us
    ppermute x1, waiting for transfers between devices, local(): lax.ppermute(parts, 'tensor', [(i, i ^ k) for i in range(cores)])  1.16 us
    ppermute x1, starting transfers between devices, local(): lax.ppermute(sent_sides, 'tensor', [(i, i ^ k) for i in range(cores)])  0.58 us
  transfers between devices with their start and end apart: 8, of which 5 were waited for; matrix products, arithmetic and copies ran while one was open for 2% of the time, Pallas kernels for 1%

profile of v6, /device:TPU:0, one launch (start us, length us, event | category | flops | bytes accessed | tf_op | source)
XLA Modules:
  0.0 22.0 jit_solution(14212364804602714587)
XLA Ops:
  0.0 0.0 copy-start
  0.0 0.0 copy-start.2
  0.0 0.0 copy-start.3
  0.0 0.0 copy-start.1
  0.0 3.0 %shard_map.82 = (f32[128,192]{1,0:T(8,128)S(1)}, bf16[128,192]{1,0:T(8,128)(2,1)S(1)}) custom-call(bf16[1,192,7168]{2,1,0:T(8,128)(2,1)} %acts.1, bf16[1,192,2048]{2,1,0:T(8,128)(2,1)} %grads.1, bf16[1,64,7168]{2,1,0:T(8,128)(2,1)} %p_in.1, bf16[1,64,2048]{2,1,0:T(8,128)(2,1)} %p_out.1), custom_call_target="tpu_custom_call" | custom-call | flops 226492416 | bytes 4718592 | tf_op jit(solution)/shard_map/pallas_call | solution.py:68
  3.0 0.6 %collective-permute-start = (bf16[128,192]{1,0:T(8,128)(2,1)S(1)}, bf16[128,192]{1,0:T(8,128)(2,1)S(1)}, u32[]{:S(2)}, u32[]{:S(2)}) collective-permute-start(bf16[128,192]{1,0:T(8,128)(2,1)S(1)} %get-tuple-element.10), channel_id=1, source_target_pairs={{0,1},{1,0},{2,3},{3,2},{4,5},{5,4},{6,7},{7,6},{8,9},{9,8},{10,11... | collective-permute-start | bytes 147464 | tf_op jit(solution)/shard_map/ppermute | solution.py:218
  3.6 0.0 copy-done
  3.6 2.7 %collective-permute-start.4 = (bf16[64,4096]{1,0:T(8,128)(2,1)S(1)}, bf16[64,4096]{1,0:T(8,128)(2,1)S(1)}, u32[]{:S(2)}, u32[]{:S(2)}) collective-permute-start(bf16[64,4096]{1,0:T(8,128)(2,1)S(1)} %bitcast.2), channel_id=1, source_target_pairs={{0,5},{1,0},{4,1},{5,4},{8,13},{9,8},{12,9},{13,12},{2,7},{3,2},{6... | collective-permute-start | bytes 1572872 | tf_op jit(solution)/shard_map/ppermute | solution.py:211
  6.2 0.0 copy-done.2
  6.2 0.1 select_reduce_fusion
  6.4 0.0 copy-done.3
  6.4 0.2 fusion.1
  6.6 0.1 select_select_fusion.bounds
  6.7 0.0 collective-permute-done.refs_1_
  6.7 0.0 copy-done.1
  6.7 0.3 %shard_map.83 = (bf16[4,4096]{1,0:T(4,128)(2,1)S(1)}, bf16[4,4096]{1,0:T(4,128)(2,1)S(1)}) custom-call(s32[8,3]{1,0:T(8,128)S(1)} %select_select_fusion.bounds, s32[1,192]{1,0:T(1,128)S(1)} %bitcast.3, f32[128,192]{1,0:T(8,128)S(1)} %get-tuple-element.9.refs_0_, bf16[128,192]{1,0:T(8,128)(2,1)S(1)} %collective-permute-done.refs_1_), custom_call_target="tpu_custom_call" | custom-call | flops 12582912 | bytes 65536 | tf_op jit(solution)/shard_map/pallas_call | solution.py:115
  7.0 1.5 %collective-permute-start.3 = (bf16[4,4096]{1,0:T(4,128)(2,1)S(1)}, bf16[4,4096]{1,0:T(4,128)(2,1)S(1)}, u32[]{:S(2)}, u32[]{:S(2)}) collective-permute-start(bf16[4,4096]{1,0:T(4,128)(2,1)S(1)} %get-tuple-element.11.refs_0_), channel_id=1, source_target_pairs={{0,9},{1,0},{4,13},{5,4},{8,1},{9,8},{12,5},{13,12},{2,11},{3,2},{... | collective-permute-start | bytes 98312 | tf_op jit(solution)/shard_map/ppermute | solution.py:242
  8.5 1.4 %collective-permute-start.2 = (bf16[4,4096]{1,0:T(4,128)(2,1)S(1)}, bf16[4,4096]{1,0:T(4,128)(2,1)S(1)}, u32[]{:S(2)}, u32[]{:S(2)}) collective-permute-start(bf16[4,4096]{1,0:T(4,128)(2,1)S(1)} %get-tuple-element.12), channel_id=1, source_target_pairs={{0,13},{1,0},{4,1},{5,4},{8,5},{9,8},{12,9},{13,12},{2,15},{3,2},{... | collective-permute-start | bytes 98312 | tf_op jit(solution)/shard_map/ppermute | solution.py:242
  9.8 0.3 %collective-permute-start.1 = (bf16[4,4096]{1,0:T(4,128)(2,1)S(1)}, bf16[4,4096]{1,0:T(4,128)(2,1)S(1)}, u32[]{:S(2)}, u32[]{:S(2)}) collective-permute-start(bf16[4,4096]{1,0:T(4,128)(2,1)S(1)} %get-tuple-element.12), channel_id=1, source_target_pairs={{0,5},{1,0},{4,9},{5,4},{8,13},{9,8},{12,1},{13,12},{2,7},{3,2},{6... | collective-permute-start | bytes 98312 | tf_op jit(solution)/shard_map/ppermute | solution.py:242
  10.2 3.1 %collective-permute-done.3.refs_3_ = bf16[4,4096]{1,0:T(4,128)(2,1)S(1)} collective-permute-done((bf16[4,4096]{1,0:T(4,128)(2,1)S(1)}, bf16[4,4096]{1,0:T(4,128)(2,1)S(1)}, u32[]{:S(2)}, u32[]{:S(2)}) %collective-permute-start.3) | collective-permute-done | bytes 32800 | tf_op jit(solution)/shard_map/ppermute | solution.py:242
  13.3 0.4 %collective-permute-done.2.refs_2_ = bf16[4,4096]{1,0:T(4,128)(2,1)S(1)} collective-permute-done((bf16[4,4096]{1,0:T(4,128)(2,1)S(1)}, bf16[4,4096]{1,0:T(4,128)(2,1)S(1)}, u32[]{:S(2)}, u32[]{:S(2)}) %collective-permute-start.2) | collective-permute-done | bytes 32800 | tf_op jit(solution)/shard_map/ppermute | solution.py:242
  13.6 0.4 %collective-permute-done.1.refs_1_ = bf16[4,4096]{1,0:T(4,128)(2,1)S(1)} collective-permute-done((bf16[4,4096]{1,0:T(4,128)(2,1)S(1)}, bf16[4,4096]{1,0:T(4,128)(2,1)S(1)}, u32[]{:S(2)}, u32[]{:S(2)}) %collective-permute-start.1) | collective-permute-done | bytes 32800 | tf_op jit(solution)/shard_map/ppermute | solution.py:242
  14.0 0.0 collective-permute-done.4.refs_5_
  14.0 3.2 %collective-permute-start.5 = (f32[2,128]{1,0:T(2,128)S(1)}, f32[2,128]{1,0:T(2,128)S(1)}, u32[]{:S(2)}, u32[]{:S(2)}) collective-permute-start(f32[2,128]{1,0:T(2,128)S(1)} %get-tuple-element.17), channel_id=1, source_target_pairs={{1,3},{0,1},{3,8},{2,0},{5,7},{4,5},{7,12},{6,4},{9,2},{8,10},{11,... | collective-permute-start | bytes 3080 | tf_op jit(solution)/shard_map/ppermute | solution.py:250
  17.2 1.2 %collective-permute-start.6 = (f32[2,128]{1,0:T(2,128)S(1)}, f32[2,128]{1,0:T(2,128)S(1)}, u32[]{:S(2)}, u32[]{:S(2)}) collective-permute-start(f32[2,128]{1,0:T(2,128)S(1)} %get-tuple-element.18), channel_id=1, source_target_pairs={{1,8},{0,1},{3,0},{2,3},{5,12},{4,5},{7,4},{6,7},{9,10},{8,9},{11,... | collective-permute-start | bytes 3080 | tf_op jit(solution)/shard_map/ppermute | solution.py:250
  18.4 0.0 collective-permute-done.5
  18.4 1.8 %collective-permute-done.6 = f32[2,128]{1,0:T(2,128)S(1)} collective-permute-done((f32[2,128]{1,0:T(2,128)S(1)}, f32[2,128]{1,0:T(2,128)S(1)}, u32[]{:S(2)}, u32[]{:S(2)}) %collective-permute-start.6) | collective-permute-done | bytes 1056 | tf_op jit(solution)/shard_map/ppermute | solution.py:250
  20.2 0.0 collective-permute-start.7
  20.2 1.2 %collective-permute-done.7 = f32[2,128]{1,0:T(2,128)S(1)} collective-permute-done((f32[2,128]{1,0:T(2,128)S(1)}, f32[2,128]{1,0:T(2,128)S(1)}, u32[]{:S(2)}, u32[]{:S(2)}) %collective-permute-start.7) | collective-permute-done | bytes 1056 | tf_op jit(solution)/shard_map/ppermute | solution.py:261
  21.4 0.6 %add.88 = f32[2,128]{1,0:T(2,128)} add(f32[2,128]{1,0:T(2,128)S(1)} %select_select_fusion.1, f32[2,128]{1,0:T(2,128)S(1)} %collective-permute-done.7) | non-fusion elementwise | flops 256 | bytes 3072 | tf_op jit(solution)/shard_map/add | solution.py:261
  (6 shorter events, 0.0 us)
Async XLA Ops:
  0.0 3.6 %copy-start = (bf16[1,64,4096]{2,1,0:T(8,128)(2,1)S(1)}, bf16[1,64,4096]{2,1,0:T(8,128)(2,1)}, u32[]{:S(2)}) copy-start(bf16[1,64,4096]{2,1,0:T(8,128)(2,1)} %refs_4_.1) | copy-start | bytes 1572868
  0.0 6.2 %copy-start.2 = (s32[8]{0:T(128)S(1)}, s32[8]{0:T(128)}, u32[]{:S(2)}) copy-start(s32[8]{0:T(128)} %param.13) | copy-start | bytes 100
  0.0 6.4 %copy-start.3 = (s32[8]{0:T(128)S(1)}, s32[8]{0:T(128)}, u32[]{:S(2)}) copy-start(s32[8]{0:T(128)} %param.14) | copy-start | bytes 100
  0.0 6.7 %copy-start.1 = (s32[192]{0:T(256)S(1)}, s32[192]{0:T(256)}, u32[]{:S(2)}) copy-start(s32[192]{0:T(256)} %param.15) | copy-start | bytes 2308
  3.0 3.7 %collective-permute-start = (bf16[128,192]{1,0:T(8,128)(2,1)S(1)}, bf16[128,192]{1,0:T(8,128)(2,1)S(1)}, u32[]{:S(2)}, u32[]{:S(2)}) collective-permute-start(bf16[128,192]{1,0:T(8,128)(2,1)S(1)} %get-tuple-element.10), channel_id=1, source_target_pairs={{0,1},{1,0},{2,3},{3,2},{4,5},{5,4},{6,7},{7,6},{8,9},{9,8},{10,11... | collective-permute-start | bytes 147464 | tf_op jit(solution)/shard_map/ppermute | solution.py:218
  3.6 10.4 %collective-permute-start.4 = (bf16[64,4096]{1,0:T(8,128)(2,1)S(1)}, bf16[64,4096]{1,0:T(8,128)(2,1)S(1)}, u32[]{:S(2)}, u32[]{:S(2)}) collective-permute-start(bf16[64,4096]{1,0:T(8,128)(2,1)S(1)} %bitcast.2), channel_id=1, source_target_pairs={{0,5},{1,0},{4,1},{5,4},{8,13},{9,8},{12,9},{13,12},{2,7},{3,2},{6... | collective-permute-start | bytes 1572872 | tf_op jit(solution)/shard_map/ppermute | solution.py:211
  7.0 6.3 %collective-permute-start.3 = (bf16[4,4096]{1,0:T(4,128)(2,1)S(1)}, bf16[4,4096]{1,0:T(4,128)(2,1)S(1)}, u32[]{:S(2)}, u32[]{:S(2)}) collective-permute-start(bf16[4,4096]{1,0:T(4,128)(2,1)S(1)} %get-tuple-element.11.refs_0_), channel_id=1, source_target_pairs={{0,9},{1,0},{4,13},{5,4},{8,1},{9,8},{12,5},{13,12},{2,11},{3,2},{... | collective-permute-start | bytes 98312 | tf_op jit(solution)/shard_map/ppermute | solution.py:242
  8.5 5.2 %collective-permute-start.2 = (bf16[4,4096]{1,0:T(4,128)(2,1)S(1)}, bf16[4,4096]{1,0:T(4,128)(2,1)S(1)}, u32[]{:S(2)}, u32[]{:S(2)}) collective-permute-start(bf16[4,4096]{1,0:T(4,128)(2,1)S(1)} %get-tuple-element.12), channel_id=1, source_target_pairs={{0,13},{1,0},{4,1},{5,4},{8,5},{9,8},{12,9},{13,12},{2,15},{3,2},{... | collective-permute-start | bytes 98312 | tf_op jit(solution)/shard_map/ppermute | solution.py:242
  9.8 4.1 %collective-permute-start.1 = (bf16[4,4096]{1,0:T(4,128)(2,1)S(1)}, bf16[4,4096]{1,0:T(4,128)(2,1)S(1)}, u32[]{:S(2)}, u32[]{:S(2)}) collective-permute-start(bf16[4,4096]{1,0:T(4,128)(2,1)S(1)} %get-tuple-element.12), channel_id=1, source_target_pairs={{0,5},{1,0},{4,9},{5,4},{8,13},{9,8},{12,1},{13,12},{2,7},{3,2},{6... | collective-permute-start | bytes 98312 | tf_op jit(solution)/shard_map/ppermute | solution.py:242
  14.0 4.4 %collective-permute-start.5 = (f32[2,128]{1,0:T(2,128)S(1)}, f32[2,128]{1,0:T(2,128)S(1)}, u32[]{:S(2)}, u32[]{:S(2)}) collective-permute-start(f32[2,128]{1,0:T(2,128)S(1)} %get-tuple-element.17), channel_id=1, source_target_pairs={{1,3},{0,1},{3,8},{2,0},{5,7},{4,5},{7,12},{6,4},{9,2},{8,10},{11,... | collective-permute-start | bytes 3080 | tf_op jit(solution)/shard_map/ppermute | solution.py:250
  17.2 3.0 %collective-permute-start.6 = (f32[2,128]{1,0:T(2,128)S(1)}, f32[2,128]{1,0:T(2,128)S(1)}, u32[]{:S(2)}, u32[]{:S(2)}) collective-permute-start(f32[2,128]{1,0:T(2,128)S(1)} %get-tuple-element.18), channel_id=1, source_target_pairs={{1,8},{0,1},{3,0},{2,3},{5,12},{4,5},{7,4},{6,7},{9,10},{8,9},{11,... | collective-permute-start | bytes 3080 | tf_op jit(solution)/shard_map/ppermute | solution.py:250
  20.2 1.2 %collective-permute-start.7 = (f32[2,128]{1,0:T(2,128)S(1)}, f32[2,128]{1,0:T(2,128)S(1)}, u32[]{:S(2)}, u32[]{:S(2)}) collective-permute-start(f32[2,128]{1,0:T(2,128)S(1)} %select_select_fusion.1), channel_id=1, source_target_pairs={{0,1},{1,0},{2,3},{3,2},{4,5},{5,4},{6,7},{7,6},{8,9},{9,8},{10,11... | collective-permute-start | bytes 3080 | tf_op jit(solution)/shard_map/ppermute | solution.py:261

commit v7 on v6

--- a/solution.py
+++ b/solution.py
@@ -23,7 +23,7 @@
     return next(n for n in (CHUNKS, 1) if depth % (n * LANES) == 0)
 
 
-def project_kernel(acts, grads, p_in, p_out, out, sent, acts_v, grads_v, in_v, out_v, sems):
+def project_kernel(acts, grads, p_in, p_out, out, acts_v, grads_v, in_v, out_v, sems):
     rank = p_out.shape[1]
     count = chunk_count(acts.shape[2])
     size = acts.shape[2] // count
@@ -57,7 +57,6 @@
         return carry
 
     lax.fori_loop(0, count, step, 0)
-    sent[...] = out[...].astype(sent.dtype)
 
 
 def project(acts, grads, p_in, p_out):
@@ -67,9 +66,9 @@
     big = [pltpu.with_memory_space_constraint(x, pltpu.HBM) for x in (acts, grads, p_in, p_out)]
     return pl.pallas_call(
         project_kernel,
-        out_shape=[jax.ShapeDtypeStruct((ranks, toks), x) for x in (jnp.float32, jnp.bfloat16)],
+        out_shape=jax.ShapeDtypeStruct((ranks, toks), jnp.float32),
         in_specs=[pl.BlockSpec(memory_space=pltpu.HBM)] * 4,
-        out_specs=[VMEM] * 2,
+        out_specs=VMEM,
         scratch_shapes=[pltpu.VMEM(x.shape[1:], x.dtype) for x in big]
         + [pltpu.SemaphoreType.DMA((2 * chunk_count(acts.shape[2]) + 2,))],
         compiler_params=pltpu.CompilerParams(vmem_limit_bytes=16 << 20),
@@ -90,7 +89,7 @@
     inside = (lane >= bounds[:, 0:1]) & (lane < bounds[:, 1:2]) & (mask[...] != 0)
     both = shares[0][...]
     for share in shares[1:]:
-        both = both + share[...].astype(jnp.float32)
+        both = both + share[...]
     both = both.astype(jnp.bfloat16)
     g, a = both[:rank_out].astype(jnp.float32), both[rank_out:]
     spread = [jnp.where(inside, g[i : i + 1], 0.0) for i in range(rank_out)]
@@ -210,12 +209,12 @@
     for k in range(1, pair):
         wanted.append(lax.ppermute(queries[0], ("dp", "tensor"), to_last(dps, cores, k)))
 
-    partial_sides, sent_sides = project(
+    partial_sides = project(
         activations, out_grads, proj_in, proj_out
     )
     shares = [partial_sides]
     for k in range(1, cores):
-        shares.append(lax.ppermute(sent_sides, "tensor", [(i, i ^ k) for i in range(cores)]))
+        shares.append(lax.ppermute(partial_sides, "tensor", [(i, i ^ k) for i in range(cores)]))
 
     rows = layers * own_rows
     index = jnp.arange(pair * rows, dtype=jnp.int32)

time: 22.1 us -> 22.1 us (level)
  no operation moved by 1% of the time
where the time goes in v7:
time: 22.1 us; the launch traced here: 21.9 us
  starting transfers between devices  11 us (50%)
  waiting for transfers between devices  6.7 us (30%)
  Pallas kernels  3.24 us (15%)
  other arithmetic  0.97 us (4%)
    ppermute x2, starting transfers between devices, local(): piece = lax.ppermute(piece, ('dp', 'layer', 'tensor'), perm)  4.42 us
    ppermute x3, waiting for transfers between devices, local(): held.append(lax.ppermute(sketches[k % pair], ('dp', 'tensor'), perm))  3.74 us
    ppermute x3, starting transfers between devices, local(): held.append(lax.ppermute(sketches[k % pair], ('dp', 'tensor'), perm))  3.3 us
    pallas_call x1, Pallas kernels, project(): pl.pallas_call(project_kernel, out_shape=jax.ShapeDtypeStruct((ranks, tok...  2.97 us
    ppermute x1, starting transfers between devices, local(): lax.ppermute(queries[0], ('dp', 'tensor'), to_last(dps, cores, k))  2.67 us
    ppermute x2, waiting for transfers between devices, local(): piece = lax.ppermute(piece, ('dp', 'layer', 'tensor'), perm)  1.79 us
    ppermute x1, waiting for transfers between devices, local(): lax.ppermute(parts, 'tensor', [(i, i ^ k) for i in range(cores)])  1.16 us
    ppermute x1, starting transfers between devices, local(): lax.ppermute(partial_sides, 'tensor', [(i, i ^ k) for i in range(cores)])  0.58 us
  transfers between devices with their start and end apart: 8, of which 5 were waited for; matrix products, arithmetic and copies ran while one was open for 2% of the time, Pallas kernels for 1%

profile of v7, /device:TPU:0, one launch (start us, length us, event | category | flops | bytes accessed | tf_op | source)
XLA Modules:
  0.0 21.9 jit_solution(3857928977951371896)
XLA Ops:
  0.0 0.0 copy-start
  0.0 0.0 copy-start.2
  0.0 0.0 copy-start.3
  0.0 0.0 copy-start.1
  0.0 3.0 %shard_map.82.refs_0_ = f32[128,192]{1,0:T(8,128)S(1)} custom-call(bf16[1,192,7168]{2,1,0:T(8,128)(2,1)} %acts.1, bf16[1,192,2048]{2,1,0:T(8,128)(2,1)} %grads.1, bf16[1,64,7168]{2,1,0:T(8,128)(2,1)} %p_in.1, bf16[1,64,2048]{2,1,0:T(8,128)(2,1)} %p_out.1), custom_call_target="tpu_custom_call" | custom-call | flops 226492416 | bytes 4718592 | tf_op jit(solution)/shard_map/pallas_call | solution.py:67
  3.0 0.6 %collective-permute-start = (f32[128,192]{1,0:T(8,128)S(1)}, f32[128,192]{1,0:T(8,128)S(1)}, u32[]{:S(2)}, u32[]{:S(2)}) collective-permute-start(f32[128,192]{1,0:T(8,128)S(1)} %shard_map.82.refs_0_), channel_id=1, source_target_pairs={{0,1},{1,0},{2,3},{3,2},{4,5},{5,4},{6,7},{7,6},{8,9},{9,8},{10,11... | collective-permute-start | bytes 294920 | tf_op jit(solution)/shard_map/ppermute | solution.py:217
  3.6 0.0 copy-done
  3.6 2.7 %collective-permute-start.4 = (bf16[64,4096]{1,0:T(8,128)(2,1)S(1)}, bf16[64,4096]{1,0:T(8,128)(2,1)S(1)}, u32[]{:S(2)}, u32[]{:S(2)}) collective-permute-start(bf16[64,4096]{1,0:T(8,128)(2,1)S(1)} %bitcast.2), channel_id=1, source_target_pairs={{0,5},{1,0},{4,1},{5,4},{8,13},{9,8},{12,9},{13,12},{2,7},{3,2},{6... | collective-permute-start | bytes 1572872 | tf_op jit(solution)/shard_map/ppermute | solution.py:210
  6.2 0.0 copy-done.2
  6.2 0.1 select_reduce_fusion
  6.4 0.0 copy-done.3
  6.4 0.2 fusion.1
  6.6 0.1 select_select_fusion.bounds
  6.7 0.0 collective-permute-done.refs_1_
  6.7 0.0 copy-done.1
  6.7 0.3 %shard_map.83 = (bf16[4,4096]{1,0:T(4,128)(2,1)S(1)}, bf16[4,4096]{1,0:T(4,128)(2,1)S(1)}) custom-call(s32[8,3]{1,0:T(8,128)S(1)} %select_select_fusion.bounds, s32[1,192]{1,0:T(1,128)S(1)} %bitcast.3, f32[128,192]{1,0:T(8,128)S(1)} %shard_map.82.refs_0_, f32[128,192]{1,0:T(8,128)S(1)} %collective-permute-done.refs_1_), custom_call_target="tpu_custom_call" | custom-call | flops 12582912 | bytes 65536 | tf_op jit(solution)/shard_map/pallas_call | solution.py:114
  6.9 1.6 %collective-permute-start.3 = (bf16[4,4096]{1,0:T(4,128)(2,1)S(1)}, bf16[4,4096]{1,0:T(4,128)(2,1)S(1)}, u32[]{:S(2)}, u32[]{:S(2)}) collective-permute-start(bf16[4,4096]{1,0:T(4,128)(2,1)S(1)} %get-tuple-element.7.refs_0_), channel_id=1, source_target_pairs={{0,9},{1,0},{4,13},{5,4},{8,1},{9,8},{12,5},{13,12},{2,11},{3,2},{... | collective-permute-start | bytes 98312 | tf_op jit(solution)/shard_map/ppermute | solution.py:241
  8.6 1.4 %collective-permute-start.2 = (bf16[4,4096]{1,0:T(4,128)(2,1)S(1)}, bf16[4,4096]{1,0:T(4,128)(2,1)S(1)}, u32[]{:S(2)}, u32[]{:S(2)}) collective-permute-start(bf16[4,4096]{1,0:T(4,128)(2,1)S(1)} %get-tuple-element.8), channel_id=1, source_target_pairs={{0,13},{1,0},{4,1},{5,4},{8,5},{9,8},{12,9},{13,12},{2,15},{3,2},{... | collective-permute-start | bytes 98312 | tf_op jit(solution)/shard_map/ppermute | solution.py:241
  9.9 0.3 %collective-permute-start.1 = (bf16[4,4096]{1,0:T(4,128)(2,1)S(1)}, bf16[4,4096]{1,0:T(4,128)(2,1)S(1)}, u32[]{:S(2)}, u32[]{:S(2)}) collective-permute-start(bf16[4,4096]{1,0:T(4,128)(2,1)S(1)} %get-tuple-element.8), channel_id=1, source_target_pairs={{0,5},{1,0},{4,9},{5,4},{8,13},{9,8},{12,1},{13,12},{2,7},{3,2},{6... | collective-permute-start | bytes 98312 | tf_op jit(solution)/shard_map/ppermute | solution.py:241
  10.2 3.0 %collective-permute-done.3.refs_3_ = bf16[4,4096]{1,0:T(4,128)(2,1)S(1)} collective-permute-done((bf16[4,4096]{1,0:T(4,128)(2,1)S(1)}, bf16[4,4096]{1,0:T(4,128)(2,1)S(1)}, u32[]{:S(2)}, u32[]{:S(2)}) %collective-permute-start.3) | collective-permute-done | bytes 32800 | tf_op jit(solution)/shard_map/ppermute | solution.py:241
  13.3 0.4 %collective-permute-done.2.refs_2_ = bf16[4,4096]{1,0:T(4,128)(2,1)S(1)} collective-permute-done((bf16[4,4096]{1,0:T(4,128)(2,1)S(1)}, bf16[4,4096]{1,0:T(4,128)(2,1)S(1)}, u32[]{:S(2)}, u32[]{:S(2)}) %collective-permute-start.2) | collective-permute-done | bytes 32800 | tf_op jit(solution)/shard_map/ppermute | solution.py:241
  13.6 0.4 %collective-permute-done.1.refs_1_ = bf16[4,4096]{1,0:T(4,128)(2,1)S(1)} collective-permute-done((bf16[4,4096]{1,0:T(4,128)(2,1)S(1)}, bf16[4,4096]{1,0:T(4,128)(2,1)S(1)}, u32[]{:S(2)}, u32[]{:S(2)}) %collective-permute-start.1) | collective-permute-done | bytes 32800 | tf_op jit(solution)/shard_map/ppermute | solution.py:241
  14.0 0.0 collective-permute-done.4.refs_5_
  14.0 3.2 %collective-permute-start.5 = (f32[2,128]{1,0:T(2,128)S(1)}, f32[2,128]{1,0:T(2,128)S(1)}, u32[]{:S(2)}, u32[]{:S(2)}) collective-permute-start(f32[2,128]{1,0:T(2,128)S(1)} %get-tuple-element.13), channel_id=1, source_target_pairs={{1,3},{0,1},{3,8},{2,0},{5,7},{4,5},{7,12},{6,4},{9,2},{8,10},{11,... | collective-permute-start | bytes 3080 | tf_op jit(solution)/shard_map/ppermute | solution.py:249
  17.2 1.2 %collective-permute-start.6 = (f32[2,128]{1,0:T(2,128)S(1)}, f32[2,128]{1,0:T(2,128)S(1)}, u32[]{:S(2)}, u32[]{:S(2)}) collective-permute-start(f32[2,128]{1,0:T(2,128)S(1)} %get-tuple-element.14), channel_id=1, source_target_pairs={{1,8},{0,1},{3,0},{2,3},{5,12},{4,5},{7,4},{6,7},{9,10},{8,9},{11,... | collective-permute-start | bytes 3080 | tf_op jit(solution)/shard_map/ppermute | solution.py:249
  18.4 0.0 collective-permute-done.5
  18.4 1.8 %collective-permute-done.6 = f32[2,128]{1,0:T(2,128)S(1)} collective-permute-done((f32[2,128]{1,0:T(2,128)S(1)}, f32[2,128]{1,0:T(2,128)S(1)}, u32[]{:S(2)}, u32[]{:S(2)}) %collective-permute-start.6) | collective-permute-done | bytes 1056 | tf_op jit(solution)/shard_map/ppermute | solution.py:249
  20.2 0.0 collective-permute-start.7
  20.2 1.2 %collective-permute-done.7 = f32[2,128]{1,0:T(2,128)S(1)} collective-permute-done((f32[2,128]{1,0:T(2,128)S(1)}, f32[2,128]{1,0:T(2,128)S(1)}, u32[]{:S(2)}, u32[]{:S(2)}) %collective-permute-start.7) | collective-permute-done | bytes 1056 | tf_op jit(solution)/shard_map/ppermute | solution.py:260
  21.4 0.6 %add.88 = f32[2,128]{1,0:T(2,128)} add(f32[2,128]{1,0:T(2,128)S(1)} %select_select_fusion.1, f32[2,128]{1,0:T(2,128)S(1)} %collective-permute-done.7) | non-fusion elementwise | flops 256 | bytes 3072 | tf_op jit(solution)/shard_map/add | solution.py:260
  (6 shorter events, 0.0 us)
Async XLA Ops:
  0.0 3.6 %copy-start = (bf16[1,64,4096]{2,1,0:T(8,128)(2,1)S(1)}, bf16[1,64,4096]{2,1,0:T(8,128)(2,1)}, u32[]{:S(2)}) copy-start(bf16[1,64,4096]{2,1,0:T(8,128)(2,1)} %refs_4_.1) | copy-start | bytes 1572868
  0.0 6.2 %copy-start.2 = (s32[8]{0:T(128)S(1)}, s32[8]{0:T(128)}, u32[]{:S(2)}) copy-start(s32[8]{0:T(128)} %param.13) | copy-start | bytes 100
  0.0 6.4 %copy-start.3 = (s32[8]{0:T(128)S(1)}, s32[8]{0:T(128)}, u32[]{:S(2)}) copy-start(s32[8]{0:T(128)} %param.14) | copy-start | bytes 100
  0.0 6.7 %copy-start.1 = (s32[192]{0:T(256)S(1)}, s32[192]{0:T(256)}, u32[]{:S(2)}) copy-start(s32[192]{0:T(256)} %param.15) | copy-start | bytes 2308
  3.0 3.7 %collective-permute-start = (f32[128,192]{1,0:T(8,128)S(1)}, f32[128,192]{1,0:T(8,128)S(1)}, u32[]{:S(2)}, u32[]{:S(2)}) collective-permute-start(f32[128,192]{1,0:T(8,128)S(1)} %shard_map.82.refs_0_), channel_id=1, source_target_pairs={{0,1},{1,0},{2,3},{3,2},{4,5},{5,4},{6,7},{7,6},{8,9},{9,8},{10,11... | collective-permute-start | bytes 294920 | tf_op jit(solution)/shard_map/ppermute | solution.py:217
  3.6 10.4 %collective-permute-start.4 = (bf16[64,4096]{1,0:T(8,128)(2,1)S(1)}, bf16[64,4096]{1,0:T(8,128)(2,1)S(1)}, u32[]{:S(2)}, u32[]{:S(2)}) collective-permute-start(bf16[64,4096]{1,0:T(8,128)(2,1)S(1)} %bitcast.2), channel_id=1, source_target_pairs={{0,5},{1,0},{4,1},{5,4},{8,13},{9,8},{12,9},{13,12},{2,7},{3,2},{6... | collective-permute-start | bytes 1572872 | tf_op jit(solution)/shard_map/ppermute | solution.py:210
  6.9 6.3 %collective-permute-start.3 = (bf16[4,4096]{1,0:T(4,128)(2,1)S(1)}, bf16[4,4096]{1,0:T(4,128)(2,1)S(1)}, u32[]{:S(2)}, u32[]{:S(2)}) collective-permute-start(bf16[4,4096]{1,0:T(4,128)(2,1)S(1)} %get-tuple-element.7.refs_0_), channel_id=1, source_target_pairs={{0,9},{1,0},{4,13},{5,4},{8,1},{9,8},{12,5},{13,12},{2,11},{3,2},{... | collective-permute-start | bytes 98312 | tf_op jit(solution)/shard_map/ppermute | solution.py:241
  8.6 5.1 %collective-permute-start.2 = (bf16[4,4096]{1,0:T(4,128)(2,1)S(1)}, bf16[4,4096]{1,0:T(4,128)(2,1)S(1)}, u32[]{:S(2)}, u32[]{:S(2)}) collective-permute-start(bf16[4,4096]{1,0:T(4,128)(2,1)S(1)} %get-tuple-element.8), channel_id=1, source_target_pairs={{0,13},{1,0},{4,1},{5,4},{8,5},{9,8},{12,9},{13,12},{2,15},{3,2},{... | collective-permute-start | bytes 98312 | tf_op jit(solution)/shard_map/ppermute | solution.py:241
  9.9 4.1 %collective-permute-start.1 = (bf16[4,4096]{1,0:T(4,128)(2,1)S(1)}, bf16[4,4096]{1,0:T(4,128)(2,1)S(1)}, u32[]{:S(2)}, u32[]{:S(2)}) collective-permute-start(bf16[4,4096]{1,0:T(4,128)(2,1)S(1)} %get-tuple-element.8), channel_id=1, source_target_pairs={{0,5},{1,0},{4,9},{5,4},{8,13},{9,8},{12,1},{13,12},{2,7},{3,2},{6... | collective-permute-start | bytes 98312 | tf_op jit(solution)/shard_map/ppermute | solution.py:241
  14.0 4.4 %collective-permute-start.5 = (f32[2,128]{1,0:T(2,128)S(1)}, f32[2,128]{1,0:T(2,128)S(1)}, u32[]{:S(2)}, u32[]{:S(2)}) collective-permute-start(f32[2,128]{1,0:T(2,128)S(1)} %get-tuple-element.13), channel_id=1, source_target_pairs={{1,3},{0,1},{3,8},{2,0},{5,7},{4,5},{7,12},{6,4},{9,2},{8,10},{11,... | collective-permute-start | bytes 3080 | tf_op jit(solution)/shard_map/ppermute | solution.py:249
  17.2 3.0 %collective-permute-start.6 = (f32[2,128]{1,0:T(2,128)S(1)}, f32[2,128]{1,0:T(2,128)S(1)}, u32[]{:S(2)}, u32[]{:S(2)}) collective-permute-start(f32[2,128]{1,0:T(2,128)S(1)} %get-tuple-element.14), channel_id=1, source_target_pairs={{1,8},{0,1},{3,0},{2,3},{5,12},{4,5},{7,4},{6,7},{9,10},{8,9},{11,... | collective-permute-start | bytes 3080 | tf_op jit(solution)/shard_map/ppermute | solution.py:249
  20.2 1.2 %collective-permute-start.7 = (f32[2,128]{1,0:T(2,128)S(1)}, f32[2,128]{1,0:T(2,128)S(1)}, u32[]{:S(2)}, u32[]{:S(2)}) collective-permute-start(f32[2,128]{1,0:T(2,128)S(1)} %select_select_fusion.1), channel_id=1, source_target_pairs={{0,1},{1,0},{2,3},{3,2},{4,5},{5,4},{6,7},{7,6},{8,9},{9,8},{10,11... | collective-permute-start | bytes 3080 | tf_op jit(solution)/shard_map/ppermute | solution.py:260
